TPU v7x, 256 devices: a whole 4x4x8 slice. The times are simulated.
256 devices in a mesh: dap: 128 (over y, x, z_hi, core), dp: 2 (over z_lo).
Axes of the slice: x: 4, y: 4, z: 8 (z_hi: 4, z_lo: 2; z = z_hi * 2 + z_lo), core: 2. Of those that a mesh axis runs over, the one named last changes fastest.
Arguments:
- pair: bfloat16 [512, 256, 128], P(('dp', 'dap')), parts along dimension 0
- token_mask: int32 [512], P('dp'), parts along dimension 0, may hold values from 0 to 1, as said below
- chain_ids: int32 [512], P('dp'), parts along dimension 0, may hold values from 0 to 3, never falling along the last dimension, each value on 1 to 128 neighbouring positions
- proj_weight: bfloat16 [128, 512], replicated
- bias_weight: bfloat16 [128, 4], replicated, may hold values from -0.5 to 0.5
- chain_weight: float32 [4], replicated, may hold values from -1.5 to 1.5
- out_weight: bfloat16 [128, 128], replicated, may hold values from -0.5 to 0.5
- cotangent: bfloat16 [512, 256, 128], P(('dp', 'dap')), parts along dimension 0, may hold values from -24 to 24
Outputs:
- next_pair_t: float32 [512, 256, 128], P(('dp', 'dap')), parts along dimension 0
- pair_grad: bfloat16 [512, 256, 128], P(('dp', 'dap')), parts along dimension 0
- proj_grad: float32 [256, 512], P('dp'), parts along dimension 0
- bias_weight_grad: float32 [256, 4], P('dp'), parts along dimension 0
- chain_grad: float32 [8], P('dp'), parts along dimension 0
- out_grad: float32 [256, 128], P('dp'), parts along dimension 0
There are 2 independent parts, one for each index of `dp`. A program takes and returns all parts, laid end to end along the dimension named above; an argument that names none is the same for every part. Nothing has to cross between parts.
Inputs may be any that keep to these rules, and one draw needn't show every extreme that they name: `token_mask`: tokens are real up to some point and padding after it; the first 128 tokens are real and the last token is padding. `chain_ids`: chain numbers never fall along the tokens; every chain has 1 to 128 tokens, one chain exactly 128.
All inputs are finite; a program needn't handle non-finite values.
Results may differ from a plain program's by a relative error of at most 0.011.
Values may be sent and summed in bfloat16 or wider, within the bound.
A program may use at most 64 MiB of HBM per device.

v0:
```python
import jax
import jax.numpy as jnp
from jax import lax
from jax.sharding import PartitionSpec as P

H = 4
DH = 32
HD = 128


epsilon = 1e-05
contract_rows = (((0,), (0,)), ((), ()))
contract_cols = (((1,), (1,)), ((), ()))


def normalize(pair):
    values_f = pair.astype(jnp.float32)
    centered = values_f - jnp.mean(values_f, axis=-1, keepdims=True)
    inverse = lax.rsqrt(jnp.mean(centered * centered, axis=-1, keepdims=True) + epsilon)
    return (centered * inverse, inverse)


def row_softmax(query_row, key_row, bias_head, extra_head):
    scores = lax.dot_general(query_row, key_row, contract_cols, preferred_element_type=jnp.float32)
    scores = scores + bias_head.astype(jnp.float32) + extra_head
    highest = jnp.max(scores, axis=1, keepdims=True)
    expo_s = jnp.exp(scores - highest)
    return expo_s / jnp.sum(expo_s, axis=1, keepdims=True)


def forward_rows(query_h, key_h, value_h, bias_head, extra_head):

    def forward_one_row(items):
        query_row, key_row, value_row = items
        attention = row_softmax(query_row, key_row, bias_head, extra_head)
        return jnp.dot(
            attention.astype(jnp.bfloat16), value_row, preferred_element_type=jnp.float32
        )

    return lax.map(forward_one_row, (query_h, key_h, value_h))


def backward_rows(query_h, key_h, value_h, grad_h, bias_head, extra_head):

    def backward_one_row(summed, items):
        query_row, key_row, value_row, grad_row = items
        attention = row_softmax(query_row, key_row, bias_head, extra_head)
        d_probs = lax.dot_general(
            grad_row, value_row, contract_cols, preferred_element_type=jnp.float32
        )
        inner_sum = jnp.sum(attention * d_probs, axis=1, keepdims=True)
        d_scores = attention * (d_probs - inner_sum)
        scores_low = d_scores.astype(jnp.bfloat16)
        d_query = jnp.dot(scores_low, key_row, preferred_element_type=jnp.float32)
        d_key = lax.dot_general(
            scores_low, query_row, contract_rows, preferred_element_type=jnp.float32
        )
        d_value = lax.dot_general(
            attention.astype(jnp.bfloat16),
            grad_row,
            contract_rows,
            preferred_element_type=jnp.float32,
        )
        return (summed + d_scores, (d_query, d_key, d_value))

    tokens = bias_head.shape[1]
    return lax.scan(
        backward_one_row,
        jnp.zeros((tokens, tokens), jnp.float32),
        (query_h, key_h, value_h, grad_h),
    )


def body(
    pair, token_mask, chain_ids, proj_weight, bias_weight, chain_weight, out_weight, cotangent
):
    row_count, length, channels = pair.shape
    standard, inverse = normalize(pair)
    normed = standard.astype(jnp.bfloat16)
    flat_x = normed.reshape(row_count * length, channels)
    projected = jnp.dot(flat_x, proj_weight, preferred_element_type=jnp.float32).reshape(
        row_count, length, 4 * HD
    )
    scaling = DH ** (-0.5)
    query = (projected[..., :HD] * scaling).astype(jnp.bfloat16)
    key_rows = projected[..., HD : 2 * HD].astype(jnp.bfloat16)
    value_rows = projected[..., 2 * HD : 3 * HD].astype(jnp.bfloat16)
    gating = jax.nn.sigmoid(projected[..., 3 * HD :])
    local_bias = jnp.dot(flat_x, bias_weight, preferred_element_type=jnp.float32).reshape(
        row_count, length, H
    )
    local_bias = jnp.transpose(local_bias, (2, 0, 1)).astype(jnp.bfloat16)
    pair_bias = lax.all_gather(local_bias, "dap", axis=1, tiled=True)
    same_chain = (chain_ids[:, None] == chain_ids[None, :]).astype(jnp.float32)
    masked = (token_mask.astype(jnp.float32) - 1.0) * 1000000000.0
    outputs = []
    for number in range(H):
        columns = slice(number * DH, (number + 1) * DH)
        extra_head = chain_weight[number] * same_chain + masked[None, :]
        outputs.append(
            forward_rows(
                query[:, :, columns],
                key_rows[:, :, columns],
                value_rows[:, :, columns],
                pair_bias[number],
                extra_head,
            )
        )
    attended = jnp.concatenate(outputs, axis=-1)
    gated = (gating * attended).astype(jnp.bfloat16)
    gated_flat = gated.reshape(row_count * length, HD)
    update = jnp.dot(gated_flat, out_weight, preferred_element_type=jnp.float32).reshape(
        row_count, length, channels
    )
    next_pair = pair.astype(jnp.float32) + update
    next_pair_t = lax.all_to_all(
        jnp.transpose(next_pair, (1, 0, 2)), "dap", split_axis=0, concat_axis=1, tiled=True
    )
    grad_flat = cotangent.reshape(row_count * length, channels)
    out_part = (
        lax.dot_general(gated_flat, grad_flat, contract_rows, preferred_element_type=jnp.float32)
        / length
    )
    d_gated = lax.dot_general(
        grad_flat, out_weight, contract_cols, preferred_element_type=jnp.float32
    ).reshape(row_count, length, HD)
    d_attended = (d_gated * gating).astype(jnp.bfloat16)
    d_gate = d_gated * attended * gating * (1.0 - gating)
    query_parts, key_parts, value_parts, totals, shares = ([], [], [], [], [])
    for number in range(H):
        columns = slice(number * DH, (number + 1) * DH)
        extra_head = chain_weight[number] * same_chain + masked[None, :]
        summed, (d_query, d_key, d_value) = backward_rows(
            query[:, :, columns],
            key_rows[:, :, columns],
            value_rows[:, :, columns],
            d_attended[:, :, columns],
            pair_bias[number],
            extra_head,
        )
        query_parts.append(d_query)
        key_parts.append(d_key)
        value_parts.append(d_value)
        totals.append(summed)
    spread = lax.psum_scatter(jnp.stack(totals, axis=0), "dap", scatter_dimension=1, tiled=True)
    bias_total = jnp.transpose(spread, (1, 2, 0))
    d_proj = jnp.concatenate(
        [
            jnp.concatenate(query_parts, axis=-1) * scaling,
            jnp.concatenate(key_parts, axis=-1),
            jnp.concatenate(value_parts, axis=-1),
            d_gate,
        ],
        axis=-1,
    ).astype(jnp.bfloat16)
    d_bias = bias_total.astype(jnp.bfloat16)
    d_proj_flat = d_proj.reshape(row_count * length, 4 * HD)
    d_bias_flat = d_bias.reshape(row_count * length, H)
    d_normed = lax.dot_general(
        d_proj_flat, proj_weight, contract_cols, preferred_element_type=jnp.float32
    )
    d_normed = d_normed + lax.dot_general(
        d_bias_flat, bias_weight, contract_cols, preferred_element_type=jnp.float32
    )
    d_normed = d_normed.reshape(row_count, length, channels)
    mean_grad = jnp.mean(d_normed, axis=-1, keepdims=True)
    mean_cross = jnp.mean(d_normed * standard, axis=-1, keepdims=True)
    pair_grad = ((d_normed - mean_grad - standard * mean_cross) * inverse).astype(jnp.bfloat16)
    proj_part = (
        lax.dot_general(flat_x, d_proj_flat, contract_rows, preferred_element_type=jnp.float32)
        / length
    )
    biasw_part = (
        lax.dot_general(flat_x, d_bias_flat, contract_rows, preferred_element_type=jnp.float32)
        / length
    )
    start_row = lax.axis_index("dap") * row_count
    local_chain = lax.dynamic_slice_in_dim(chain_ids, start_row, row_count)
    same_local = (local_chain[:, None] == chain_ids[None, :]).astype(jnp.float32)
    chain_part = jnp.sum(bias_total * same_local[:, :, None], axis=(0, 1)) / length
    proj_grad, bias_weight_grad, chain_grad, out_grad = lax.psum(
        (proj_part, biasw_part, chain_part, out_part), "dap"
    )
    return (next_pair_t, pair_grad, proj_grad, bias_weight_grad, chain_grad, out_grad)


def solution(mesh):
    return jax.shard_map(
        body,
        mesh=mesh,
        in_specs=(
            P(("dp", "dap"), None, None),
            P("dp"),
            P("dp"),
            P(),
            P(),
            P(),
            P(),
            P(("dp", "dap"), None, None),
        ),
        out_specs=(
            P(("dp", "dap"), None, None),
            P(("dp", "dap"), None, None),
            P("dp", None),
            P("dp", None),
            P("dp"),
            P("dp", None),
        ),
        check_vma=False,
    )
```

profile of v0, /device:TPU:1, one launch (start us, length us, event | category | flops | bytes accessed | tf_op | source)
XLA Modules:
  0.0 1956.5 jit_solution(10141085470042809085)
XLA Ops:
  7.2 1.1 convert_reduce_fusion
  9.9 198.1 %all_gather.3 = bf16[4,256,256]{2,0,1:T(4,128)(2,1)S(1)} all-gather(bf16[4,2,256]{2,0,1:T(4,128)(2,1)S(1)} %fusion.179), channel_id=1, replica_groups=mesh['dap'=128,'dp'=2] {'dap'}, dimensions={1}, use_global_device_ids=true | all-gather | bytes 528384 | tf_op jit(solution)/shard_map/all_gather | solution.py:93
  208.0 1.4 fusion.218
  209.5 0.8 copy.153
  211.5 1.2 fusion.217
  213.4 5.6 while.115
  213.4 1.7 fusion.320
  215.1 0.8 copy-done.27
  216.2 1.7 fusion.320
  217.9 0.8 copy-done.27
  219.1 0.8 copy-done.4
  219.9 0.8 copy.152
  220.7 5.7 while.114
  220.7 1.8 fusion.316
  222.5 0.8 copy-done.22
  223.6 1.8 fusion.316
  225.4 0.8 copy-done.22
  226.4 0.8 copy.98
  228.2 3.6 while.113
  228.2 1.5 fusion.312
  230.0 1.5 fusion.312
  233.3 3.7 while.112
  233.3 1.6 fusion.308
  235.2 1.5 fusion.308
  237.7 0.8 copy.96
  238.5 1.9 multiply_convert_fusion
  240.7 0.9 copy.100
  241.6 5.3 all-to-all-start
  250.8 0.8 fusion.178
  251.7 0.9 fusion.219
  253.3 12.2 while.119
  253.3 1.5 fusion.365
  254.9 0.8 copy-done.28
  255.7 0.8 multiply_reduce_fusion.12
  256.6 0.9 fusion.367
  259.4 1.4 fusion.365
  260.9 0.8 copy-done.28
  261.8 0.8 multiply_reduce_fusion.12
  262.6 0.9 fusion.367
  266.3 8.8 while.118
  266.3 1.8 fusion.353
  268.2 0.8 copy-done.46
  270.7 1.8 fusion.353
  272.6 0.8 copy-done.46
  276.5 8.3 while.117
  276.5 1.6 fusion.341
  278.2 0.8 copy-done.44
  280.7 1.5 fusion.341
  282.3 0.8 copy-done.44
  285.7 6.9 while.116
  285.7 1.5 fusion.329
  287.3 0.8 copy-done.43
  289.1 1.6 fusion.329
  290.8 0.8 copy-done.43
  295.7 0.8 copy.144
  296.5 0.8 copy.143
  297.3 0.8 copy.142
  300.9 1.1 fusion.176
  302.0 2.0 pad_maximum_fusion
  308.2 0.8 copy.101
  309.0 1288.4 %all-reduce.5.cloned.1.call-done = (f32[4,256,256]{2,0,1:T(4,128)}, f32[128,512]{1,0:T(8,128)}, f32[128,128]{1,0:T(8,128)}) async-done(((f32[4,256,256]{2,0,1:T(4,128)}, f32[128,512]{1,0:T(8,128)}, f32[128,128]{1,0:T(8,128)}), (f32[4,256,256]{2,0,1:T(4,128)}, f32[128,512]{1,0:T(8,128)}, f32[128,128]{1,0:T(8,128)})) %all-reduce.5.cloned.1.call-update) | async-done | bytes 1376272
  1599.8 0.8 multiply_reduce_fusion.4
  1600.7 1.0 fusion.189
  1601.7 346.5 %all-reduce.1 = (f32[128,4]{0,1:T(4,128)}, f32[4]{0:T(128)}) all-reduce(f32[128,4]{0,1:T(4,128)S(1)} %fusion.180, f32[4]{0:T(128)S(1)} %broadcast_multiply_fusion.3), channel_id=1, replica_groups=mesh['dap'=128,'dp'=2] {'dap'}, use_global_device_ids=true, to_apply=%region_42.43 | all-reduce | flops 516 | bytes 4128 | tf_op jit(solution)/shard_map/psum | solution.py:181
  (280 shorter events, 43.1 us)
Async XLA Ops:
  7.2 1.4 copy-start
  7.2 1.1 copy-start.1
  209.5 0.8 copy-start.52
  215.0 0.9 copy-start.27
  217.8 0.9 copy-start.27
  219.0 0.9 copy-start.4
  222.5 0.9 copy-start.22
  225.3 0.9 copy-start.22
  226.4 0.8 copy-start.2
  227.3 0.9 copy-start.18
  232.4 0.9 copy-start.16
  233.3 5.2 copy-start.41
  237.0 1.5 copy-start.56
  237.0 1.5 copy-start.14
  237.7 0.8 copy-start.51
  241.6 66.6 %all-to-all-start = ((f32[256,2,128]{2,1,0:T(2,128)}), f32[256,2,128]{2,1,0:T(2,128)S(1)}, u32[]{:S(2)}, u32[]{:S(2)}) async-start(f32[256,2,128]{2,1,0:T(2,128)} %copy.100), calls=%async_computation | async-start | bytes 524288 | tf_op jit(solution)/shard_map/all_to_all | solution.py:116
  246.9 1350.5 %all-reduce.5.cloned.1.call-start = ((), (), s32[]{:S(2)}) async-start(), calls=%async_computation.1 | async-start | bytes 2752512
  248.4 2.4 copy-start.42
  251.7 0.9 copy-start.26
  253.3 12.8 copy-start.3
  253.3 12.8 copy-start.23
  254.8 0.9 copy-start.28
  254.8 1.0 copy-start.48
  257.6 0.9 copy-start.49
  258.7 0.7 copy-start.58
  260.9 0.9 copy-start.28
  260.9 1.0 copy-start.48
  263.7 0.9 copy-start.49
  264.8 0.7 copy-start.58
  265.5 0.8 copy-start.8
  265.5 0.8 copy-start.33
  265.5 0.8 copy-start.36
  266.3 10.0 copy-start.19
  266.3 10.0 copy-start.25
  268.1 0.9 copy-start.46
  269.6 0.9 copy-start.47
  272.5 0.9 copy-start.46
  274.0 0.9 copy-start.47
  275.7 0.8 copy-start.31
  275.7 0.8 copy-start.32
  276.5 8.4 copy-start.17
  276.5 8.4 copy-start.21
  278.1 0.9 copy-start.44
  279.6 0.9 copy-start.45
  282.2 0.9 copy-start.44
  283.7 0.9 copy-start.45
  284.8 0.8 copy-start.10
  284.9 0.8 copy-start.29
  284.9 0.8 copy-start.30
  287.2 0.9 copy-start.43
  290.7 0.9 copy-start.43
  292.7 0.8 copy-start.35
  293.9 0.8 copy-start.38
  294.6 0.8 copy-start.40
  297.3 0.8 copy-start.9
  298.3 0.8 copy-start.11
  299.4 0.9 copy-start.12
  300.9 1.1 copy-start.5
  300.9 1.1 copy-start.6
  300.9 1.1 copy-start.7
  304.6 0.9 copy-start.13
  1598.4 0.7 copy-start.54
  1600.7 347.5 %copy-start.15 = (f32[128,512]{1,0:T(8,128)S(1)}, f32[128,512]{1,0:T(8,128)}, u32[]{:S(2)}) copy-start(f32[128,512]{1,0:T(8,128)} %get-tuple-element.2116) | copy-start | bytes 786436
  1948.1 0.9 copy-start.50
  (10 other events, 6.5 us)
Sparse Core Ops, SparseCore 0:
  304.1 1293.2 all-reduce.4
where the time goes:
time: 1960 us
  waiting for transfers between devices  1290 us (66%)
  blocking collectives  545 us (28%)
  local copies, waits for them, and re-layouts  51.2 us (3%)
  matrix products  40.6 us (2%)
    unnamed x2, waiting for transfers between devices  1290 us
    psum x1, blocking collectives, body(): lax.psum((proj_part, biasw_part, chain_part, out_part), 'dap')  346 us
    all_gather x1, blocking collectives, body(): pair_bias = lax.all_gather(local_bias, 'dap', axis=1, tiled=True)  198 us
  transfers between devices with their start and end apart: 2, of which 1 were waited for; matrix products, arithmetic and copies ran while one was open for 2% of the time, Pallas kernels for 0%

commit v1 on v0

v1 whole, which is shorter than its diff:
```python
import functools

import jax
import jax.numpy as jnp
from jax import lax
from jax.experimental import pallas as pl
from jax.experimental.pallas import tpu as pltpu
from jax.sharding import PartitionSpec as P

H = 4
DH = 32
HD = 128
C = 128
GRID = (4, 4, 4, 2)
EPSILON = 1e-05

F32 = jnp.float32
BF16 = jnp.bfloat16
NN = (((1,), (0,)), ((), ()))
NT = (((1,), (1,)), ((), ()))
TN = (((0,), (0,)), ((), ()))


def dot(a, b, dims=NN):
    return lax.dot_general(a, b, dims, preferred_element_type=F32)


def kernel(
    grid,
    tokens,
    cw_ref,
    pair_ref,
    mask_ref,
    chain_ref,
    w_ref,
    bw_ref,
    ow_ref,
    cot_ref,
    npt_ref,
    pg_ref,
    wg_ref,
    small_ref,
    std_ref,
    inv_ref,
    normed_ref,
    q_ref,
    k_ref,
    v_ref,
    da_ref,
    qt_ref,
    dat_ref,
    gate_ref,
    dgated_ref,
    att_ref,
    dq_ref,
    dkt_ref,
    dvt_ref,
    same_ref,
    dbias_ref,
    dproj_ref,
    slot_ref,
    bias_ref,
    sc_ref,
    rc_ref,
    sa_ref,
    ra_ref,
    sb_ref,
    rb_ref,
    sz_ref,
    rz_ref,
    wsc_ref,
    wrc_ref,
    wsa_ref,
    wra_ref,
    wrb_ref,
    wrz_ref,
    wag_ref,
    us_ref,
    ua_ref,
    ub_ref,
    ux_ref,
    uz_ref,
    ur_ref,
    t0_ref,
    t1_ref,
    t2_ref,
    slot_s,
    slot_r,
    ag_s,
    ag_r,
    agc_s,
    agc_r,
    rsc_s,
    rsc_r,
    rsa_s,
    rsa_r,
    rsb_s,
    rsb_r,
    rsz_s,
    rsz_r,
    wc_s,
    wc_r,
    wa_s,
    wa_r,
    wb_s,
    wb_r,
    wz_s,
    wz_r,
    wga_s,
    wga_r,
    wgc_s,
    wgc_r,
    ua_s,
    ua_r,
    ub_s,
    ub_r,
    uz_s,
    uz_r,
    t0_s,
    t0_r,
    t1_s,
    t1_r,
    t2_s,
    t2_r,
):
    NY, NX, NZ, NC = grid
    G = NZ * NC
    NB = NX * NY
    NA = NX
    BR = 2 * G
    N = tokens
    T = 2 * N
    HC = H // NC
    WR = C // NC // NA

    idx = lax.axis_index("dap")
    zc = lax.rem(idx, G)
    c = lax.rem(idx, NC)
    z = lax.div(zc, NC)
    yx = lax.div(idx, G)
    x = lax.rem(yx, NX)
    y = lax.div(yx, NX)
    a_me = x + (y - x) * c
    b_me = y + (x - y) * c
    a_stride = G + (G * NX - G) * c
    b_stride = G * NX - (G * NX - G) * c
    partner = idx + 1 - 2 * c
    far = HC * (1 - c)
    near = HC * c

    def blk(a, b):
        return a * (1 + (NX - 1) * c) + b * (NX - (NX - 1) * c)

    def zc_peer(g):
        return idx + g - zc

    def a_peer(a):
        return idx + (a - a_me) * a_stride

    def b_peer(b):
        return idx + (b - b_me) * b_stride

    def z_peer(zz):
        return idx + (zz - z) * NC

    def x_peer(xx):
        return idx + (xx - x) * G

    def y_peer(yy):
        return idx + (yy - y) * G * NX

    def others(me, n):
        return [lax.rem(me + d, n) for d in range(1, n)]

    def copy(src, dst, ssem, rsem, dev):
        return pltpu.make_async_remote_copy(
            src_ref=src,
            dst_ref=dst,
            send_sem=ssem,
            recv_sem=rsem,
            device_id={"dap": dev},
            device_id_type=pl.DeviceIdType.MESH,
        )

    barrier = pltpu.get_barrier_semaphore()
    peers = [zc_peer(g) for g in others(zc, G)]
    peers += [x_peer(v) for v in others(x, NX)]
    peers += [y_peer(v) for v in others(y, NY)]
    for p in peers:
        pl.semaphore_signal(
            barrier, inc=1, device_id={"dap": p}, device_id_type=pl.DeviceIdType.MESH
        )

    values = pair_ref[...].reshape(T, C).astype(F32)
    centered = values - jnp.mean(values, axis=-1, keepdims=True)
    inverse = lax.rsqrt(jnp.mean(centered * centered, axis=-1, keepdims=True) + EPSILON)
    standard = centered * inverse
    std_ref[...] = standard
    inv_ref[...] = jnp.broadcast_to(inverse, (T, C))
    normed = standard.astype(BF16)
    normed_ref[...] = normed
    bwt = jnp.transpose(bw_ref[...].astype(F32)).astype(BF16)
    local_bias = dot(bwt, normed, NT)
    slot_ref[zc] = jnp.concatenate(
        [local_bias[0:H, 0:N], local_bias[0:H, N:T]], axis=0
    ).astype(BF16)

    pl.semaphore_wait(barrier, len(peers))
    slot_out = []
    for g in others(zc, G):
        d = copy(slot_ref.at[zc], slot_ref.at[zc], slot_s.at[g], slot_r.at[zc], zc_peer(g))
        d.start()
        slot_out.append(d)

    def arrived(ref, sem):
        copy(ref, ref, sem, sem, partner).wait_recv()

    projected = dot(normed, w_ref[...])
    scaling = DH ** (-0.5)
    q = (projected[:, 0:HD] * scaling).astype(BF16)
    q_ref[...] = q
    k_ref[...] = projected[:, HD : 2 * HD].astype(BF16)
    v_ref[...] = projected[:, 2 * HD : 3 * HD].astype(BF16)
    gating = jax.nn.sigmoid(projected[:, 3 * HD :])
    gate_ref[...] = gating

    for g in others(zc, G):
        arrived(slot_ref.at[g], slot_r.at[g])
    gathered = slot_ref[...].reshape(G * 2 * H, N)
    for t in range(HC):
        at = lax.broadcasted_iota(jnp.int32, (BR, G * 2 * H), 0) * H + (far + t)
        pick = (at == lax.broadcasted_iota(jnp.int32, (BR, G * 2 * H), 1)).astype(BF16)
        bias_ref[far + t, yx] = dot(pick, gathered).astype(BF16)

    ag_out = []

    def ag_send(number, block, dev, ssem, rsem):
        part = bias_ref.at[pl.ds(far, HC), block]
        d = copy(part, part, ssem.at[number], rsem.at[block], dev)
        d.start()
        ag_out.append(d)

    number = 0
    for b in others(b_me, NA):
        ag_send(number, yx, b_peer(b), ag_s, ag_r)
        number += 1
    for a in others(a_me, NA):
        ag_send(number, yx, a_peer(a), ag_s, ag_r)
        number += 1
    ag_send(yx, yx, partner, agc_s, agc_r)

    grad = cot_ref[...].reshape(T, C)
    d_gated = dot(grad, ow_ref[...], NT)
    dgated_ref[...] = d_gated
    da32 = d_gated * gating
    da_ref[...] = da32.astype(BF16)
    for r in range(2):
        rows = slice(r * N, (r + 1) * N)
        qt_ref[r] = jnp.transpose(projected[rows, 0:HD] * scaling).astype(BF16)
        dat_ref[r] = jnp.transpose(da32[rows]).astype(BF16)
    chain = chain_ref[...].astype(F32)
    chain_cols = jnp.transpose(jnp.broadcast_to(chain, (HD, N)))
    chain_cols = jnp.concatenate([chain_cols] * (-(-N // HD)), axis=1)[:, 0:N]
    same_ref[...] = (chain_cols == jnp.broadcast_to(chain, (N, N))).astype(F32)

    def landed(block, sem):
        part = bias_ref.at[pl.ds(far, HC), block]
        copy(part, part, sem.at[block], sem.at[block], partner).wait_recv()

    for b in others(b_me, NA):
        block = blk(a_me, b)
        landed(block, ag_r)
        for a in others(a_me, NA):
            ag_send(number, block, a_peer(a), ag_s, ag_r)
            number += 1
        ag_send(block, block, partner, agc_s, agc_r)
    for a in others(a_me, NA):
        for b in range(NA):
            block = blk(a, b)
            landed(block, ag_r)
            ag_send(block, block, partner, agc_s, agc_r)

    masked = (mask_ref[...].astype(F32) - 1.0) * 1000000000.0
    head_of = lax.broadcasted_iota(jnp.int32, (N, HD), 1) // DH
    att_ref[...] = jnp.zeros((2, N, HD), F32)
    dq_ref[...] = jnp.zeros((2, N, HD), F32)

    def one_head(h):
        own = head_of == h
        none = jnp.zeros((N, HD), BF16)
        extra = cw_ref[h] * same_ref[...] + masked
        bias = bias_ref[h].reshape(N, N).astype(F32)
        head_rows = pl.ds(pl.multiple_of(h * DH, DH), DH)
        for r in range(2):
            rows = slice(r * N, (r + 1) * N)
            k_row, v_row = k_ref[rows, :], v_ref[rows, :]
            scores = dot(jnp.where(own, q_ref[rows, :], none), k_row, NT)
            scores = scores + bias + extra
            expo = jnp.exp(scores - jnp.max(scores, axis=1, keepdims=True))
            probs = expo * (1.0 / jnp.sum(expo, axis=1, keepdims=True))
            probs_low = probs.astype(BF16)
            att_ref[r] += dot(probs_low, jnp.where(own, v_row, none))
            d_probs = dot(jnp.where(own, da_ref[rows, :], none), v_row, NT)
            inner = jnp.sum(probs * d_probs, axis=1, keepdims=True)
            d_scores = probs * (d_probs - inner)
            low = d_scores.astype(BF16)
            dq_ref[r] += dot(low, jnp.where(own, k_row, none))
            dkt_ref[r, head_rows, :] = dot(qt_ref[r, head_rows, :], low)
            dvt_ref[r, head_rows, :] = dot(dat_ref[r, head_rows, :], probs_low)
            if r == 0:
                dbias_ref[h] = d_scores
            else:
                dbias_ref[h] += d_scores


    def far_landed():
        for a in range(NA):
            for b in range(NA):
                block = blk(a, b)
                part = bias_ref.at[pl.ds(near, HC), block]
                sem = agc_r.at[block]
                copy(part, part, sem, sem, partner).wait_recv()

    def rsc(t):
        return copy(sc_ref.at[t], rc_ref.at[t], rsc_s.at[t], rsc_r.at[t], partner)

    @pl.loop(0, HC)
    def _(t):
        one_head(far + t)
        sc_ref[t] = dbias_ref[far + t].reshape(NB, BR, N).astype(BF16)
        rsc(t).start()

    far_landed()

    @pl.loop(0, HC)
    def _(t):
        one_head(near + t)

    for t in range(HC):
        rsc(t).wait_recv()
        total = dbias_ref[near + t] + rc_ref[t].reshape(N, N).astype(F32)
        sa_ref[t] = total.reshape(NB, BR, N).astype(BF16)
    rsa_out = []
    number = 0
    for a in others(a_me, NA):
        for b in range(NA):
            d = copy(
                sa_ref.at[:, blk(a, b)],
                ra_ref.at[a_me, b],
                rsa_s.at[number],
                rsa_r.at[a_me * NA + b],
                a_peer(a),
            )
            d.start()
            rsa_out.append(d)
            number += 1

    attended = att_ref[...].reshape(T, HD)
    gating = gate_ref[...]
    gated = (gating * attended).astype(BF16)
    grad = cot_ref[...].reshape(T, C)
    update = dot(gated, ow_ref[...])
    next_pair = pair_ref[...].reshape(T, C).astype(F32) + update
    us_ref[...] = next_pair.astype(BF16).reshape(2, NB, BR, C)
    ua_out = []
    number = 0
    for a in others(a_me, NA):
        for b in range(NA):
            d = copy(
                us_ref.at[:, blk(a, b)],
                ua_ref.at[a_me, b],
                ua_s.at[number],
                ua_r.at[a_me * NA + b],
                a_peer(a),
            )
            d.start()
            ua_out.append(d)
            number += 1

    d_gate = dgated_ref[...] * attended * gating * (1.0 - gating)
    dproj_ref[:, 0:HD] = (dq_ref[...].reshape(T, HD) * scaling).astype(BF16)
    for r in range(2):
        rows = slice(r * N, (r + 1) * N)
        dproj_ref[rows, HD : 2 * HD] = jnp.transpose(dkt_ref[r]).astype(BF16)
        dproj_ref[rows, 2 * HD : 3 * HD] = jnp.transpose(dvt_ref[r]).astype(BF16)
    dproj_ref[:, 3 * HD :] = d_gate.astype(BF16)
    normed = normed_ref[...]
    proj_part = dot(normed, dproj_ref[...], TN)
    out_part = dot(gated, grad, TN)
    half = C // NC
    wfull_ref = wag_ref
    wsum = jnp.concatenate([proj_part, out_part], axis=1).reshape(NC, half, 5 * HD)
    wfull_ref[...] = wsum.astype(BF16).reshape(NC, NA, WR, 5 * HD)
    wsc_ref[...] = wfull_ref[1 - c]
    wc = copy(wsc_ref, wrc_ref, wc_s, wc_r, partner)
    wc.start()

    for b in range(NA):
        arrived_rows = sa_ref[:, blk(a_me, b)].astype(F32)
        for a in others(a_me, NA):
            arrived(ra_ref.at[a, b], rsa_r.at[a * NA + b])
            arrived_rows = arrived_rows + ra_ref[a, b].astype(F32)
        sb_ref[b] = arrived_rows.astype(BF16)
    rsb_out = []
    for number, b in enumerate(others(b_me, NA)):
        d = copy(sb_ref.at[b], rb_ref.at[b_me], rsb_s.at[number], rsb_r.at[b_me], b_peer(b))
        d.start()
        rsb_out.append(d)

    ua_ref[a_me] = jnp.stack([us_ref[:, blk(a_me, b)] for b in range(NA)], axis=0)
    for a in others(a_me, NA):
        for b in range(NA):
            arrived(ua_ref.at[a, b], ua_r.at[a * NA + b])
    ub_out = []
    number = 0
    for b in others(b_me, NA):
        for a in range(NA):
            d = copy(
                ua_ref.at[a, b],
                ub_ref.at[blk(a, b_me)],
                ub_s.at[number],
                ub_r.at[blk(a, b_me)],
                b_peer(b),
            )
            d.start()
            ub_out.append(d)
            number += 1
    for a in range(NA):
        ub_ref[blk(a, b_me)] = ua_ref[a, b_me]

    wc.wait()
    own_rows = wfull_ref[c].astype(F32) + wrc_ref[...].astype(F32)
    wsa_ref[...] = own_rows.astype(BF16)
    wa_out = []
    for number, a in enumerate(others(a_me, NA)):
        d = copy(wsa_ref.at[a], wra_ref.at[a_me], wa_s.at[number], wa_r.at[a_me], a_peer(a))
        d.start()
        wa_out.append(d)
    wra_ref[a_me] = wsa_ref[a_me]

    total = sb_ref[b_me].astype(F32)
    for b in others(b_me, NA):
        arrived(rb_ref.at[b], rsb_r.at[b])
        total = total + rb_ref[b].astype(F32)
    for g in range(G):
        for jl in range(2):
            sz_ref[g, jl * HC : (jl + 1) * HC, :] = total[:, 2 * g + jl, :]
    rsz_out = []
    for g in others(zc, G):
        d = copy(sz_ref.at[g], rz_ref.at[zc], rsz_s.at[g], rsz_r.at[zc], zc_peer(g))
        d.start()
        rsz_out.append(d)
    rz_ref[zc] = sz_ref[zc]

    for a in others(a_me, NA):
        arrived(wra_ref.at[a], wa_r.at[a])
    wsum = wra_ref[0].astype(F32)
    for a in range(1, NA):
        wsum = wsum + wra_ref[a].astype(F32)
    wrb_ref[b_me] = wsum.astype(BF16)
    wb_out = []
    for number, b in enumerate(others(b_me, NA)):
        d = copy(wrb_ref.at[b_me], wrb_ref.at[b_me], wb_s.at[number], wb_r.at[b_me], b_peer(b))
        d.start()
        wb_out.append(d)

    for b in others(b_me, NA):
        for a in range(NA):
            block = blk(a, b)
            arrived(ub_ref.at[block], ub_r.at[block])
    ux_ref[...] = ub_ref[...].reshape(NB * 2 * BR, C).astype(F32)
    for g in range(G):
        for jl in range(2):
            for r in range(2):
                start = r * BR + 2 * g + jl
                uz_ref[g, jl, r] = ux_ref[pl.ds(start, NB, stride=2 * BR), :].astype(BF16)
    uz_out = []
    for g in others(zc, G):
        d = copy(uz_ref.at[g], ur_ref.at[zc], uz_s.at[g], uz_r.at[zc], zc_peer(g))
        d.start()
        uz_out.append(d)
    ur_ref[zc] = uz_ref[zc]

    d_normed = dot(dproj_ref[...], w_ref[...], NT)

    for b in others(b_me, NA):
        arrived(wrb_ref.at[b], wb_r.at[b])
    wsum = wrb_ref[0].astype(F32)
    for b in range(1, NA):
        wsum = wsum + wrb_ref[b].astype(F32)
    wrz_ref[z] = wsum.astype(BF16)
    wz_out = []
    for number, zz in enumerate(others(z, NZ)):
        d = copy(wrz_ref.at[z], wrz_ref.at[z], wz_s.at[number], wz_r.at[z], z_peer(zz))
        d.start()
        wz_out.append(d)

    for g in others(zc, G):
        arrived(rz_ref.at[g], rsz_r.at[g])
    sums = []
    for core in range(NC):
        part = rz_ref[core]
        for zz in range(1, NZ):
            part = part + rz_ref[zz * NC + core]
        sums.append(part)
    d_bias = []
    for jl in range(2):
        d_bias.append(
            jnp.concatenate([s[jl * HC : (jl + 1) * HC] for s in sums], axis=0)
        )
    d_bias = jnp.concatenate(d_bias, axis=1)
    d_bias = jnp.concatenate([d_bias, jnp.zeros((8 - H, T), F32)], axis=0).astype(BF16)
    small = dot(d_bias, normed_ref[...])
    lane = lax.broadcasted_iota(jnp.int32, (8, C), 1)
    row = lax.broadcasted_iota(jnp.int32, (8, C), 0)
    for h in range(H):
        value = jnp.sum(dbias_ref[h] * same_ref[...], axis=0, keepdims=True)
        value = jnp.sum(value, axis=1, keepdims=True)
        small = jnp.where((row == H) & (lane == h), value, small)

    def exchange(mine, me, n, ref, ssem, rsem, peer):
        ref[me] = mine
        outs = []
        for other in others(me, n):
            d = copy(ref.at[me], ref.at[me], ssem.at[other], rsem.at[me], peer(other))
            d.start()
            outs.append(d)
        return outs

    def collect(me, n, ref, rsem):
        for other in others(me, n):
            arrived(ref.at[other], rsem.at[other])
        out = ref[0]
        for other in range(1, n):
            out = out + ref[other]
        return out

    t0_out = exchange(small, zc, G, t0_ref, t0_s, t0_r, zc_peer)

    bwt = jnp.transpose(bw_ref[...].astype(F32)).astype(BF16)
    d_normed = d_normed + dot(d_bias, bwt, TN)
    standard = std_ref[...]
    mean_grad = jnp.mean(d_normed, axis=-1, keepdims=True)
    mean_cross = jnp.mean(d_normed * standard, axis=-1, keepdims=True)
    pair_grad = (d_normed - mean_grad - standard * mean_cross) * inv_ref[...]
    pg_ref[...] = pair_grad.astype(BF16).reshape(2, N, C)

    small = collect(zc, G, t0_ref, t0_r)
    t1_out = exchange(small, y, NY, t1_ref, t1_s, t1_r, y_peer)

    for zz in others(z, NZ):
        arrived(wrz_ref.at[zz], wz_r.at[zz])
    wsum = wrz_ref[0].astype(F32)
    for zz in range(1, NZ):
        wsum = wsum + wrz_ref[zz].astype(F32)
    wag_ref[c, a_me] = wsum.astype(BF16)
    wga_out = []
    wgc_out = []

    def pass_on(a):
        part = wag_ref.at[c, a]
        d = copy(part, part, wgc_s.at[a], wgc_r.at[a], partner)
        d.start()
        wgc_out.append(d)

    for number, a in enumerate(others(a_me, NA)):
        part = wag_ref.at[c, a_me]
        d = copy(part, part, wga_s.at[number], wga_r.at[a_me], a_peer(a))
        d.start()
        wga_out.append(d)
    pass_on(a_me)

    for g in others(zc, G):
        arrived(ur_ref.at[g], uz_r.at[g])
    for g in range(G):
        for jl in range(2):
            for r in range(2):
                start = jl * N + 2 * g + r
                npt_ref[pl.ds(start, NB, stride=BR), :] = ur_ref[g, jl, r].astype(F32)

    small = collect(y, NY, t1_ref, t1_r)
    t2_out = exchange(small, x, NX, t2_ref, t2_s, t2_r, x_peer)

    for a in others(a_me, NA):
        arrived(wag_ref.at[c, a], wga_r.at[a])
        pass_on(a)
    for a in range(NA):
        arrived(wag_ref.at[1 - c, a], wgc_r.at[a])
    wg_ref[...] = wag_ref[...].reshape(C, 5 * HD).astype(F32) * (1.0 / N)

    small = collect(x, NX, t2_ref, t2_r)
    small_ref[...] = small * (1.0 / N)

    for d in (
        slot_out + ag_out + rsa_out + ua_out + rsb_out + ub_out + wa_out + rsz_out
        + wb_out + uz_out + wz_out + t0_out + t1_out + wga_out + wgc_out + t2_out
    ):
        d.wait_send()
    for t in range(HC):
        rsc(t).wait_send()


def scratch(grid, N):
    NY, NX, NZ, NC = grid
    G, NB, NA, HC = NZ * NC, NX * NY, NX, H // NC
    BR, T, WR = 2 * G, 2 * N, C // NC // NX
    V = pltpu.VMEM
    buffers = [
        V((T, C), F32),
        V((T, C), F32),
        V((T, C), BF16),
        V((T, HD), BF16),
        V((T, HD), BF16),
        V((T, HD), BF16),
        V((T, HD), BF16),
        V((2, HD, N), BF16),
        V((2, HD, N), BF16),
        V((T, HD), F32),
        V((T, HD), F32),
        V((2, N, HD), F32),
        V((2, N, HD), F32),
        V((2, HD, N), F32),
        V((2, HD, N), F32),
        V((N, N), F32),
        V((H, N, N), F32),
        V((T, 4 * HD), BF16),
        V((G, 2 * H, N), BF16),
        V((H, NB, BR, N), BF16),
        V((HC, NB, BR, N), BF16),
        V((HC, NB, BR, N), BF16),
        V((HC, NB, BR, N), BF16),
        V((NA, NA, HC, BR, N), BF16),
        V((NA, HC, BR, N), BF16),
        V((NA, HC, BR, N), BF16),
        V((G, 2 * HC, N), F32),
        V((G, 2 * HC, N), F32),
        V((NA, WR, 5 * HD), BF16),
        V((NA, WR, 5 * HD), BF16),
        V((NA, WR, 5 * HD), BF16),
        V((NA, WR, 5 * HD), BF16),
        V((NA, WR, 5 * HD), BF16),
        V((NZ, WR, 5 * HD), BF16),
        V((NC, NA, WR, 5 * HD), BF16),
        V((2, NB, BR, C), BF16),
        V((NA, NA, 2, BR, C), BF16),
        V((NB, 2, BR, C), BF16),
        V((NB * 2 * BR, C), F32),
        V((G, 2, 2, NB, C), BF16),
        V((G, 2, 2, NB, C), BF16),
        V((G, 8, C), F32),
        V((NY, 8, C), F32),
        V((NX, 8, C), F32),
    ]
    dma = pltpu.SemaphoreType.DMA
    counts = [
        (G, G),
        ((NA - 1) * (NA + 1), NB),
        (NB, NB),
        (HC, HC),
        ((NA - 1) * NA, NB),
        (NA - 1, NA),
        (G, G),
        (None, None),
        (NA - 1, NA),
        (NA - 1, NA),
        (NZ - 1, NZ),
        (NA - 1, NA),
        (NA, NA),
        ((NA - 1) * NA, NB),
        ((NA - 1) * NA, NB),
        (G, G),
        (G, G),
        (NY, NY),
        (NX, NX),
    ]
    for pair in counts:
        for n in pair:
            buffers.append(dma if n is None else dma((n,)))
    return buffers


def body(
    grid, pair, token_mask, chain_ids, proj_weight, bias_weight, chain_weight, out_weight, cotangent
):
    N = pair.shape[1]
    vmem = pl.BlockSpec(memory_space=pltpu.VMEM)
    smem = pl.BlockSpec(memory_space=pltpu.SMEM)
    bias_padded = jnp.pad(bias_weight, ((0, 0), (0, 8 - H)))
    npt, pair_grad, weights, small = pl.pallas_call(
        functools.partial(kernel, grid, N),
        out_shape=(
            jax.ShapeDtypeStruct((2 * N, C), F32),
            jax.ShapeDtypeStruct((2, N, C), BF16),
            jax.ShapeDtypeStruct((C, 5 * HD), F32),
            jax.ShapeDtypeStruct((8, C), F32),
        ),
        in_specs=[smem] + [vmem] * 7,
        out_specs=(vmem,) * 4,
        scratch_shapes=scratch(grid, N),
        compiler_params=pltpu.CompilerParams(collective_id=0, has_side_effects=True),
    )(
        chain_weight,
        pair,
        token_mask.reshape(1, N),
        chain_ids.reshape(1, N),
        proj_weight,
        bias_padded,
        out_weight,
        cotangent,
    )
    return (
        npt.reshape(2, N, C),
        pair_grad,
        weights[:, 0 : 4 * HD],
        jnp.transpose(small[0:H, :]),
        small[H, 0:H],
        weights[:, 4 * HD :],
    )


def solution(mesh, grid=GRID):
    return jax.shard_map(
        functools.partial(body, grid),
        mesh=mesh,
        in_specs=(
            P(("dp", "dap"), None, None),
            P("dp"),
            P("dp"),
            P(),
            P(),
            P(),
            P(),
            P(("dp", "dap"), None, None),
        ),
        out_specs=(
            P(("dp", "dap"), None, None),
            P(("dp", "dap"), None, None),
            P("dp", None),
            P("dp", None),
            P("dp"),
            P("dp", None),
        ),
        check_vma=False,
    )
```

time: 1960 us -> 67.3 us (0.03)
  waiting for transfers between devices: 1290 us -> 0 us
  blocking collectives: 545 us -> 0 us
  Pallas kernels: 0 us -> 58.3 us
  local copies, waits for them, and re-layouts: 51.2 us -> 8.03 us
  matrix products: 40.6 us -> 0 us
    unnamed x2 -> x0, waiting for transfers between devices: 1290 us -> none
    psum x1 -> x0, blocking collectives: 346 us -> none  [body(): lax.psum((proj_part, biasw_part, chain_part, out_part), 'dap')]
    all_gather x1 -> x0, blocking collectives: 198 us -> none  [body(): pair_bias = lax.all_gather(local_bias, 'dap', axis=1, tiled=True)]
    pallas_call x0 -> x1, Pallas kernels: none -> 58.3 us  [body(): pl.pallas_call(functools.partial(kernel, grid, N), out_shape=(jax.ShapeDt...]
    dot_general x65 -> x0, matrix products: 40.6 us -> none  [the longest x16 25.8 us: row_softmax(): lax.dot_general(query_row, key_row, contract_cols, preferred_element_type...]
  transfers between devices with their start and end apart: 2 -> 0, of which waited for: 1 -> 0; matrix products, arithmetic and copies ran while one was open for 2% -> 0% of each run, Pallas kernels for 0% -> 0%
where the time goes in v1:
time: 67.3 us; the launch traced here: 67 us
  Pallas kernels  58.3 us (87%)
  local copies, waits for them, and re-layouts  8.03 us (12%)
    pallas_call x1, Pallas kernels, body(): pl.pallas_call(functools.partial(kernel, grid, N), out_shape=(jax.ShapeDt...  58.3 us
    unnamed x11, local copies, waits for them, and re-layouts  3.13 us
    slice x1, local copies, waits for them, and re-layouts, body(): weights[:, 0:4 * HD]  1.71 us
    slice x1, local copies, waits for them, and re-layouts, body(): weights[:, 4 * HD:]  1.47 us

profile of v1, /device:TPU:1, one launch (start us, length us, event | category | flops | bytes accessed | tf_op | source)
XLA Modules:
  0.0 67.0 jit_solution(13320273540123289565)
XLA Ops:
  0.6 0.0 copy-start.2
  0.6 0.7 copy-done.2
  1.3 0.1 copy.14
  1.4 0.6 pad.4.bw_ref
  2.1 58.3 %shard_map.127 = (f32[512,128]{1,0:T(8,128)}, bf16[2,256,128]{2,1,0:T(8,128)(2,1)}, f32[128,640]{1,0:T(8,128)}, f32[8,128]{1,0:T(8,128)}) custom-call(f32[4]{0:T(128)} %cw_ref.1, bf16[2,256,128]{2,1,0:T(8,128)(2,1)} %pair_ref.1, s32[1,256]{1,0:T(1,128)} %bitcast.8, s32[1,256]{1,0:T(1,128)} %bitcast.9, bf16[128,512]{1,0:T(8,128)(2,1)} %w_ref.1, ...), custom_call_target="tpu_custom_call" | custom-call | tf_op jit(solution)/shard_map/pallas_call | solution.py:689
  60.4 0.0 copy-start.3
  60.4 0.7 copy-done.3
  61.1 0.5 slice_bitcast_fusion.1
  61.6 0.6 slice_bitcast_fusion
  62.2 1.5 %slice.15 = f32[128,128]{1,0:T(8,128)} slice(f32[128,640]{1,0:T(8,128)} %get-tuple-element.12), slice={[0:128], [512:640]} | slice | bytes 131072 | tf_op jit(solution)/shard_map/slice | solution.py:717
  63.7 0.0 copy-start
  63.7 1.7 %slice.12 = f32[128,512]{1,0:T(8,128)} slice(f32[128,640]{1,0:T(8,128)} %get-tuple-element.12), slice={[0:128], [0:512]} | slice | bytes 524288 | tf_op jit(solution)/shard_map/slice | solution.py:714
  65.4 0.0 copy-done
  65.4 0.0 copy-start.1
  65.4 0.7 %copy.17 = f32[2,256,128]{2,1,0:T(8,128)} copy(f32[2,256,128]{2,1,0:T(8,128)S(1)} %bitcast.7) | data formatting | bytes 524288
  66.1 0.3 copy-done.1
  66.4 0.7 copy.18
Async XLA Ops:
  0.6 0.7 %copy-start.2 = (bf16[128,4]{0,1:T(4,128)(2,1)S(1)}, bf16[128,4]{0,1:T(4,128)(2,1)}, u32[]{:S(2)}) copy-start(bf16[128,4]{0,1:T(4,128)(2,1)} %param.12) | copy-start | bytes 3076
  60.4 0.7 %copy-start.3 = (f32[8,128]{1,0:T(8,128)S(1)}, f32[8,128]{1,0:T(8,128)}, u32[]{:S(2)}) copy-start(f32[8,128]{1,0:T(8,128)} %get-tuple-element.13) | copy-start | bytes 12292
  63.7 1.7 %copy-start = (f32[512,128]{1,0:T(8,128)S(1)}, f32[512,128]{1,0:T(8,128)}, u32[]{:S(2)}) copy-start(f32[512,128]{1,0:T(8,128)} %get-tuple-element.10) | copy-start | bytes 786436
  65.4 1.0 %copy-start.1 = (bf16[2,256,128]{2,1,0:T(8,128)(2,1)S(1)}, bf16[2,256,128]{2,1,0:T(8,128)(2,1)}, u32[]{:S(2)}) copy-start(bf16[2,256,128]{2,1,0:T(8,128)(2,1)} %get-tuple-element.21) | copy-start | bytes 393220

commit v2 on v1

v2 whole, which is shorter than its diff:
```python
import functools

import jax
import jax.numpy as jnp
from jax import lax
from jax.experimental import pallas as pl
from jax.experimental.pallas import tpu as pltpu
from jax.sharding import PartitionSpec as P

H = 4
DH = 32
HD = 128
C = 128
GRID = (4, 4, 4, 2)
EPSILON = 1e-05

F32 = jnp.float32
BF16 = jnp.bfloat16
NN = (((1,), (0,)), ((), ()))
NT = (((1,), (1,)), ((), ()))
TN = (((0,), (0,)), ((), ()))


def dot(a, b, dims=NN):
    return lax.dot_general(a, b, dims, preferred_element_type=F32)


def kernel(
    grid,
    tokens,
    cw_hbm,
    pair_hbm,
    mask_hbm,
    chain_hbm,
    w_hbm,
    bw_hbm,
    ow_hbm,
    cot_hbm,
    npt_o,
    pg_o,
    wag_o,
    small_o,
    cw_ref,
    pair_ref,
    mask_ref,
    chain_ref,
    w_ref,
    bw_ref,
    ow_ref,
    cot_ref,
    npt_ref,
    pg_ref,
    small_ref,
    std_ref,
    inv_ref,
    normed_ref,
    q_ref,
    k_ref,
    v_ref,
    da_ref,
    qt_ref,
    dat_ref,
    gate_ref,
    dgated_ref,
    att_ref,
    dq_ref,
    dkt_ref,
    dvt_ref,
    same_ref,
    dbias_ref,
    dproj_ref,
    s0_ref,
    dp_ref,
    slot_ref,
    bias_ref,
    sc_ref,
    rc_ref,
    sa_ref,
    ra_ref,
    sz_ref,
    rz_ref,
    wfull_ref,
    wrc_ref,
    wsa_ref,
    wra_ref,
    wrz_ref,
    wag_ref,
    us_ref,
    ub_ref,
    ux_ref,
    uz_ref,
    ur_ref,
    t0_ref,
    t1_ref,
    in_s,
    out_s,
    slot_s,
    slot_r,
    ag_s,
    ag_r,
    agc_s,
    agc_r,
    rsc_s,
    rsc_r,
    rsa_s,
    rsa_r,
    rsz_s,
    rsz_r,
    wc_s,
    wc_r,
    wa_s,
    wa_r,
    wz_s,
    wz_r,
    wga_s,
    wga_r,
    wgc_s,
    wgc_r,
    ua_s,
    ua_r,
    uz_s,
    uz_r,
    t0_s,
    t0_r,
    t1_s,
    t1_r,
):
    NY, NX, NZ, NC = grid
    G = NZ * NC
    NB = NX * NY
    BR = 2 * G
    N = tokens
    T = 2 * N
    HC = H // NC

    idx = lax.axis_index("dap")
    zc = lax.rem(idx, G)
    c = lax.rem(idx, NC)
    z = lax.div(zc, NC)
    yx = lax.div(idx, G)
    x = lax.rem(yx, NX)
    y = lax.div(yx, NX)
    partner = idx + 1 - 2 * c
    far = HC * (1 - c)
    near = HC * c

    def zc_peer(g):
        return idx + g - zc

    def yx_peer(b):
        return idx + (b - yx) * G

    def z_peer(zz):
        return idx + (zz - z) * NC

    def others(me, n):
        return [lax.rem(me + d, n) for d in range(1, n)]

    steps = [(i, j) for i in range(NY) for j in range(NX) if i or j]
    steps.sort(key=lambda s: -min(s[0], NY - s[0]) - min(s[1], NX - s[1]))
    plane = [lax.rem(y + i, NY) * NX + lax.rem(x + j, NX) for i, j in steps]
    column = others(zc, G)

    def copy(src, dst, ssem, rsem, dev):
        return pltpu.make_async_remote_copy(
            src_ref=src,
            dst_ref=dst,
            send_sem=ssem,
            recv_sem=rsem,
            device_id={"dap": dev},
            device_id_type=pl.DeviceIdType.MESH,
        )

    sent = []

    def send(src, dst, ssem, rsem, dev):
        d = copy(src, dst, ssem, rsem, dev)
        d.start()
        sent.append(d)

    def arrived(ref, sem):
        copy(ref, ref, sem, sem, partner).wait_recv()

    barrier = pltpu.get_barrier_semaphore()
    peers = [yx_peer(b) for b in plane] + [zc_peer(g) for g in column]
    for p in peers:
        pl.semaphore_signal(
            barrier, inc=1, device_id={"dap": p}, device_id_type=pl.DeviceIdType.MESH
        )

    loads = []
    for number, (src, dst) in enumerate(
        (
            (pair_hbm, pair_ref),
            (bw_hbm, bw_ref),
            (w_hbm, w_ref),
            (cot_hbm, cot_ref),
            (ow_hbm, ow_ref),
            (chain_hbm, chain_ref),
            (mask_hbm, mask_ref),
            (cw_hbm, cw_ref),
        )
    ):
        d = pltpu.make_async_copy(src, dst, in_s.at[number])
        d.start()
        loads.append(d)
    loads[0].wait()

    values = pair_ref[...].reshape(T, C).astype(F32)
    centered = values - jnp.mean(values, axis=-1, keepdims=True)
    inverse = lax.rsqrt(jnp.mean(centered * centered, axis=-1, keepdims=True) + EPSILON)
    standard = centered * inverse
    std_ref[...] = standard
    inv_ref[...] = jnp.broadcast_to(inverse, (T, C))
    normed = standard.astype(BF16)
    normed_ref[...] = normed
    loads[1].wait()
    bwt = jnp.concatenate([bw_ref[...].astype(F32), jnp.zeros((8 - H, C), F32)], axis=0)
    bwt = bwt.astype(BF16)
    local_bias = dot(bwt, normed, NT)
    slot_ref[zc] = jnp.concatenate(
        [local_bias[0:H, 0:N], local_bias[0:H, N:T]], axis=0
    ).astype(BF16)

    pl.semaphore_wait(barrier, len(peers))
    for g in column:
        send(slot_ref.at[zc], slot_ref.at[zc], slot_s.at[g], slot_r.at[zc], zc_peer(g))

    for d in loads[2:]:
        d.wait()
    projected = dot(normed, w_ref[...])
    scaling = DH ** (-0.5)
    q32 = projected[:, 0:HD] * scaling
    q_ref[...] = q32.astype(BF16)
    k_ref[...] = projected[:, HD : 2 * HD].astype(BF16)
    v_ref[...] = projected[:, 2 * HD : 3 * HD].astype(BF16)
    gating = jax.nn.sigmoid(projected[:, 3 * HD :])
    gate_ref[...] = gating
    d_gated = dot(cot_ref[...].reshape(T, C), ow_ref[...], NT)
    dgated_ref[...] = d_gated
    da32 = d_gated * gating
    da_ref[...] = da32.astype(BF16)
    for r in range(2):
        rows = slice(r * N, (r + 1) * N)
        qt_ref[r] = jnp.transpose(q32[rows]).astype(BF16)
        dat_ref[r] = jnp.transpose(da32[rows]).astype(BF16)

    for g in column:
        arrived(slot_ref.at[g], slot_r.at[g])
    gathered = slot_ref[...].reshape(G * 2 * H, N)
    for t in range(HC):
        at = lax.broadcasted_iota(jnp.int32, (BR, G * 2 * H), 0) * H + (far + t)
        pick = (at == lax.broadcasted_iota(jnp.int32, (BR, G * 2 * H), 1)).astype(BF16)
        bias_ref[far + t, yx] = dot(pick, gathered).astype(BF16)

    def bias_block(first, block):
        return bias_ref.at[pl.ds(first, HC), block]

    def hand_over(block):
        part = bias_block(far, block)
        send(part, part, agc_s.at[block], agc_r.at[block], partner)

    for number, b in enumerate(plane):
        part = bias_block(far, yx)
        send(part, part, ag_s.at[number], ag_r.at[yx], yx_peer(b))
    hand_over(yx)

    chain = chain_ref[...].astype(F32)
    chain_cols = jnp.transpose(jnp.broadcast_to(chain, (HD, N)))
    chain_cols = jnp.concatenate([chain_cols] * (-(-N // HD)), axis=1)[:, 0:N]
    same_ref[...] = (chain_cols == jnp.broadcast_to(chain, (N, N))).astype(F32)
    masked = (mask_ref[...].astype(F32) - 1.0) * 1000000000.0
    head_of = lax.broadcasted_iota(jnp.int32, (N, HD), 1) // DH
    none = jnp.zeros((N, HD), BF16)

    @pl.loop(0, H)
    def _(h):
        own = head_of == h
        lane = lax.broadcasted_iota(jnp.int32, (1, H), 1) == h
        weight = jnp.sum(jnp.where(lane, cw_ref[...], 0.0), axis=1, keepdims=True)
        extra = weight * same_ref[...] + masked
        for r in range(2):
            rows = slice(r * N, (r + 1) * N)
            products = dot(jnp.where(own, q_ref[rows, :], none), k_ref[rows, :], NT)
            s0_ref[r, h] = products + extra
            dp_ref[r, h] = dot(jnp.where(own, da_ref[rows, :], none), v_ref[rows, :], NT)

    for b in plane:
        arrived(bias_block(far, b), ag_r.at[b])
        hand_over(b)

    att_ref[...] = jnp.zeros((2, N, HD), F32)
    dq_ref[...] = jnp.zeros((2, N, HD), F32)

    def one_head(h):
        own = head_of == h
        bias = bias_ref[h].reshape(N, N).astype(F32)
        head_rows = pl.ds(pl.multiple_of(h * DH, DH), DH)
        for r in range(2):
            rows = slice(r * N, (r + 1) * N)
            scores = s0_ref[r, h] + bias
            expo = jnp.exp(scores - jnp.max(scores, axis=1, keepdims=True))
            probs = expo * (1.0 / jnp.sum(expo, axis=1, keepdims=True))
            probs_low = probs.astype(BF16)
            att_ref[r] += dot(probs_low, jnp.where(own, v_ref[rows, :], none))
            d_probs = dp_ref[r, h]
            inner = jnp.sum(probs * d_probs, axis=1, keepdims=True)
            d_scores = probs * (d_probs - inner)
            low = d_scores.astype(BF16)
            dq_ref[r] += dot(low, jnp.where(own, k_ref[rows, :], none))
            dkt_ref[r, head_rows, :] = dot(qt_ref[r, head_rows, :], low)
            dvt_ref[r, head_rows, :] = dot(dat_ref[r, head_rows, :], probs_low)
            if r == 0:
                dbias_ref[h] = d_scores
            else:
                dbias_ref[h] += d_scores

    def rsc(t):
        return copy(sc_ref.at[t], rc_ref.at[t], rsc_s.at[t], rsc_r.at[t], partner)

    @pl.loop(0, HC)
    def _(t):
        one_head(far + t)
        sc_ref[t] = dbias_ref[far + t].reshape(NB, BR, N).astype(BF16)
        rsc(t).start()

    for b in [yx] + plane:
        arrived(bias_block(near, b), agc_r.at[b])

    def plane_copy(t, number):
        b = plane[number]
        return copy(
            sa_ref.at[t, b],
            ra_ref.at[yx, t],
            rsa_s.at[t, number],
            rsa_r.at[t, yx],
            yx_peer(b),
        )

    @pl.loop(0, HC)
    def _(t):
        one_head(near + t)
        rsc(t).wait_recv()
        total = dbias_ref[near + t] + rc_ref[t].reshape(N, N).astype(F32)
        sa_ref[t] = total.reshape(NB, BR, N).astype(BF16)
        for number in range(NB - 1):
            plane_copy(t, number).start()

    attended = att_ref[...].reshape(T, HD)
    gating = gate_ref[...]
    gated = (gating * attended).astype(BF16)
    update = dot(gated, ow_ref[...])
    next_pair = pair_ref[...].reshape(T, C).astype(F32) + update
    us_ref[...] = next_pair.astype(BF16).reshape(2, NB, BR, C)
    for number, b in enumerate(plane):
        send(us_ref.at[:, b], ub_ref.at[yx], ua_s.at[number], ua_r.at[yx], yx_peer(b))
    ub_ref[yx] = us_ref[:, yx]

    d_gate = dgated_ref[...] * attended * gating * (1.0 - gating)
    dproj_ref[:, 0:HD] = (dq_ref[...].reshape(T, HD) * scaling).astype(BF16)
    for r in range(2):
        rows = slice(r * N, (r + 1) * N)
        dproj_ref[rows, HD : 2 * HD] = jnp.transpose(dkt_ref[r]).astype(BF16)
        dproj_ref[rows, 2 * HD : 3 * HD] = jnp.transpose(dvt_ref[r]).astype(BF16)
    dproj_ref[:, 3 * HD :] = d_gate.astype(BF16)
    proj_part = dot(normed_ref[...], dproj_ref[...], TN)
    out_part = dot(gated, cot_ref[...].reshape(T, C), TN)
    wfull_ref[0] = proj_part[:, 0 : 3 * HD].reshape(16, 8, 3 * HD).astype(BF16)
    wfull_ref[1, :, :, 0:HD] = proj_part[:, 3 * HD :].reshape(16, 8, HD).astype(BF16)
    wfull_ref[1, :, :, HD : 2 * HD] = out_part.reshape(16, 8, HD).astype(BF16)
    wfull_ref[1, :, :, 2 * HD :] = jnp.zeros((16, 8, HD), BF16)
    wc = copy(wfull_ref.at[1 - c], wrc_ref, wc_s, wc_r, partner)
    wc.start()

    chain_sums = jnp.zeros((8, C), F32)
    lane = lax.broadcasted_iota(jnp.int32, (8, C), 1)
    row = lax.broadcasted_iota(jnp.int32, (8, C), 0)
    for h in range(H):
        value = jnp.sum(dbias_ref[h] * same_ref[...], axis=0, keepdims=True)
        value = jnp.sum(value, axis=1, keepdims=True)
        chain_sums = jnp.where((row == H) & (lane == h), value, chain_sums)

    total = sa_ref[:, yx].astype(F32)
    for b in plane:
        for t in range(HC):
            arrived(ra_ref.at[b, t], rsa_r.at[t, b])
        total = total + ra_ref[b].astype(F32)
    for g in range(G):
        for jl in range(2):
            sz_ref[g, jl * HC : (jl + 1) * HC, :] = total[:, 2 * g + jl, :]
    for g in column:
        send(sz_ref.at[g], rz_ref.at[zc], rsz_s.at[g], rsz_r.at[zc], zc_peer(g))
    rz_ref[zc] = sz_ref[zc]

    wc.wait()
    own_half = wfull_ref[c].astype(F32) + wrc_ref[...].astype(F32)
    wsa_ref[...] = own_half.reshape(NB, 128 // NB, 3 * HD).astype(BF16)
    for number, b in enumerate(plane):
        send(wsa_ref.at[b], wra_ref.at[yx], wa_s.at[number], wa_r.at[yx], yx_peer(b))
    wra_ref[yx] = wsa_ref[yx]

    for b in plane:
        arrived(ub_ref.at[b], ua_r.at[b])
    ux_ref[...] = ub_ref[...].reshape(NB * 2 * BR, C).astype(F32)
    for g in range(G):
        for jl in range(2):
            for r in range(2):
                start = r * BR + 2 * g + jl
                uz_ref[g, jl, r] = ux_ref[pl.ds(start, NB, stride=2 * BR), :].astype(BF16)
    for g in column:
        send(uz_ref.at[g], ur_ref.at[zc], uz_s.at[g], uz_r.at[zc], zc_peer(g))
    ur_ref[zc] = uz_ref[zc]

    d_normed = dot(dproj_ref[...], w_ref[...], NT)

    for b in plane:
        arrived(wra_ref.at[b], wa_r.at[b])
    wsum = wra_ref[0].astype(F32)
    for b in range(1, NB):
        wsum = wsum + wra_ref[b].astype(F32)
    wrz_ref[z] = wsum.astype(BF16)
    for number, zz in enumerate(others(z, NZ)):
        send(wrz_ref.at[z], wrz_ref.at[z], wz_s.at[number], wz_r.at[z], z_peer(zz))

    for g in column:
        arrived(rz_ref.at[g], rsz_r.at[g])
    sums = []
    for core in range(NC):
        part = rz_ref[core]
        for zz in range(1, NZ):
            part = part + rz_ref[zz * NC + core]
        sums.append(part)
    d_bias = []
    for jl in range(2):
        d_bias.append(
            jnp.concatenate([s[jl * HC : (jl + 1) * HC] for s in sums], axis=0)
        )
    d_bias = jnp.concatenate(d_bias, axis=1)
    d_bias = jnp.concatenate([d_bias, jnp.zeros((8 - H, T), F32)], axis=0).astype(BF16)

    t0_ref[zc] = dot(d_bias, normed_ref[...]) + chain_sums
    for g in column:
        send(t0_ref.at[zc], t0_ref.at[zc], t0_s.at[g], t0_r.at[zc], zc_peer(g))

    d_normed = d_normed + dot(d_bias, bwt, TN)
    standard = std_ref[...]
    mean_grad = jnp.mean(d_normed, axis=-1, keepdims=True)
    mean_cross = jnp.mean(d_normed * standard, axis=-1, keepdims=True)
    pair_grad = (d_normed - mean_grad - standard * mean_cross) * inv_ref[...]
    pg_ref[...] = pair_grad.astype(BF16)
    pg_out = pltpu.make_async_copy(pg_ref, pg_o, out_s.at[0])
    pg_out.start()

    for g in column:
        arrived(ur_ref.at[g], uz_r.at[g])
    for g in range(G):
        for jl in range(2):
            for r in range(2):
                start = jl * N + 2 * g + r
                npt_ref[pl.ds(start, NB, stride=BR), :] = ur_ref[g, jl, r].astype(F32)
    npt_out = pltpu.make_async_copy(npt_ref, npt_o, out_s.at[1])
    npt_out.start()

    for zz in others(z, NZ):
        arrived(wrz_ref.at[zz], wz_r.at[zz])
    wsum = wrz_ref[0].astype(F32)
    for zz in range(1, NZ):
        wsum = wsum + wrz_ref[zz].astype(F32)
    wag_ref[c, yx] = wsum.astype(BF16)

    def pass_on(b):
        part = wag_ref.at[c, b]
        send(part, part, wgc_s.at[b], wgc_r.at[b], partner)

    for number, b in enumerate(plane):
        part = wag_ref.at[c, yx]
        send(part, part, wga_s.at[number], wga_r.at[yx], yx_peer(b))
    pass_on(yx)

    for g in column:
        arrived(t0_ref.at[g], t0_r.at[g])
    small = t0_ref[0]
    for g in range(1, G):
        small = small + t0_ref[g]
    t1_ref[yx] = small
    for number, b in enumerate(plane):
        send(t1_ref.at[yx], t1_ref.at[yx], t1_s.at[number], t1_r.at[yx], yx_peer(b))

    for b in plane:
        arrived(wag_ref.at[c, b], wga_r.at[b])
        pass_on(b)
    for b in [yx] + plane:
        arrived(wag_ref.at[1 - c, b], wgc_r.at[b])
    wag_out = pltpu.make_async_copy(wag_ref, wag_o, out_s.at[2])
    wag_out.start()

    for b in plane:
        arrived(t1_ref.at[b], t1_r.at[b])
    small = t1_ref[0]
    for b in range(1, NB):
        small = small + t1_ref[b]
    small_ref[...] = small * (1.0 / N)
    small_out = pltpu.make_async_copy(small_ref, small_o, out_s.at[3])
    small_out.start()

    for d in sent:
        d.wait_send()
    for t in range(HC):
        rsc(t).wait_send()
        for number in range(NB - 1):
            plane_copy(t, number).wait_send()
    for d in (pg_out, npt_out, wag_out, small_out):
        d.wait()


def scratch(grid, N):
    NY, NX, NZ, NC = grid
    G, NB, HC = NZ * NC, NX * NY, H // NC
    BR, T, WR = 2 * G, 2 * N, 128 // NB
    V = pltpu.VMEM
    buffers = [
        V((1, H), F32),
        V((2, N, C), BF16),
        V((1, N), jnp.int32),
        V((1, N), jnp.int32),
        V((C, 4 * HD), BF16),
        V((H, C), BF16),
        V((HD, C), BF16),
        V((2, N, C), BF16),
        V((T, C), F32),
        V((T, C), BF16),
        V((8, C), F32),
        V((T, C), F32),
        V((T, C), F32),
        V((T, C), BF16),
        V((T, HD), BF16),
        V((T, HD), BF16),
        V((T, HD), BF16),
        V((T, HD), BF16),
        V((2, HD, N), BF16),
        V((2, HD, N), BF16),
        V((T, HD), F32),
        V((T, HD), F32),
        V((2, N, HD), F32),
        V((2, N, HD), F32),
        V((2, HD, N), F32),
        V((2, HD, N), F32),
        V((N, N), F32),
        V((H, N, N), F32),
        V((T, 4 * HD), BF16),
        V((2, H, N, N), F32),
        V((2, H, N, N), F32),
        V((G, 2 * H, N), BF16),
        V((H, NB, BR, N), BF16),
        V((HC, NB, BR, N), BF16),
        V((HC, NB, BR, N), BF16),
        V((HC, NB, BR, N), BF16),
        V((NB, HC, BR, N), BF16),
        V((G, 2 * HC, N), F32),
        V((G, 2 * HC, N), F32),
        V((NC, 16, 8, 3 * HD), BF16),
        V((16, 8, 3 * HD), BF16),
        V((NB, WR, 3 * HD), BF16),
        V((NB, WR, 3 * HD), BF16),
        V((NZ, WR, 3 * HD), BF16),
        V((NC, NB, WR, 3 * HD), BF16),
        V((2, NB, BR, C), BF16),
        V((NB, 2, BR, C), BF16),
        V((NB * 2 * BR, C), F32),
        V((G, 2, 2, NB, C), BF16),
        V((G, 2, 2, NB, C), BF16),
        V((G, 8, C), F32),
        V((NB, 8, C), F32),
    ]
    dma = pltpu.SemaphoreType.DMA
    counts = [
        ((8,), (4,)),
        ((G,), (G,)),
        ((NB,), (NB,)),
        ((NB,), (NB,)),
        ((HC,), (HC,)),
        ((HC, NB), (HC, NB)),
        ((G,), (G,)),
        (None, None),
        ((NB,), (NB,)),
        ((NZ,), (NZ,)),
        ((NB,), (NB,)),
        ((NB,), (NB,)),
        ((NB,), (NB,)),
        ((G,), (G,)),
        ((G,), (G,)),
        ((NB,), (NB,)),
    ]
    for both in counts:
        for shape in both:
            buffers.append(dma if shape is None else dma(shape))
    return buffers


def finish(npt_ref, pg_ref, wag_ref, small_ref, npt_o, pg_o, wg_o, bg_o, cg_o, og_o):
    N = npt_o.shape[1]
    npt_o[...] = npt_ref[...].reshape(2, N, C)
    pg_o[...] = pg_ref[...].reshape(2, N, C)
    scale = 1.0 / N
    first = wag_ref[0].astype(F32).reshape(C, 3 * HD) * scale
    second = wag_ref[1].astype(F32).reshape(C, 3 * HD) * scale
    wg_o[:, 0 : 3 * HD] = first
    wg_o[:, 3 * HD :] = second[:, 0:HD]
    og_o[...] = second[:, HD : 2 * HD]
    bg_o[...] = small_ref[0:H, :]
    cg_o[...] = small_ref[H : H + 1, 0:H]


def body(
    grid, pair, token_mask, chain_ids, proj_weight, bias_weight, chain_weight, out_weight, cotangent
):
    N = pair.shape[1]
    NY, NX, NZ, NC = grid
    vmem = pl.BlockSpec(memory_space=pltpu.VMEM)
    hbm = pl.BlockSpec(memory_space=pl.ANY)
    results = pl.pallas_call(
        functools.partial(kernel, grid, N),
        out_shape=(
            jax.ShapeDtypeStruct((2 * N, C), F32),
            jax.ShapeDtypeStruct((2 * N, C), BF16),
            jax.ShapeDtypeStruct((NC, NX * NY, 128 // (NX * NY), 3 * HD), BF16),
            jax.ShapeDtypeStruct((8, C), F32),
        ),
        in_specs=[hbm] * 8,
        out_specs=(hbm,) * 4,
        scratch_shapes=scratch(grid, N),
        compiler_params=pltpu.CompilerParams(collective_id=0, has_side_effects=True),
    )(
        chain_weight.reshape(1, H),
        pair,
        token_mask.reshape(1, N),
        chain_ids.reshape(1, N),
        proj_weight,
        jnp.transpose(bias_weight),
        out_weight,
        cotangent,
    )
    npt, pair_grad, weight_grad, bias_grad, chain_grad, out_grad = pl.pallas_call(
        finish,
        out_shape=(
            jax.ShapeDtypeStruct((2, N, C), F32),
            jax.ShapeDtypeStruct((2, N, C), BF16),
            jax.ShapeDtypeStruct((C, 4 * HD), F32),
            jax.ShapeDtypeStruct((H, C), F32),
            jax.ShapeDtypeStruct((1, H), F32),
            jax.ShapeDtypeStruct((HD, C), F32),
        ),
        in_specs=[vmem] * 4,
        out_specs=(vmem,) * 6,
    )(*results)
    return (
        npt,
        pair_grad,
        weight_grad,
        jnp.transpose(bias_grad),
        chain_grad.reshape(H),
        out_grad,
    )


def solution(mesh, grid=GRID):
    return jax.shard_map(
        functools.partial(body, grid),
        mesh=mesh,
        in_specs=(
            P(("dp", "dap"), None, None),
            P("dp"),
            P("dp"),
            P(),
            P(),
            P(),
            P(),
            P(("dp", "dap"), None, None),
        ),
        out_specs=(
            P(("dp", "dap"), None, None),
            P(("dp", "dap"), None, None),
            P("dp", None),
            P("dp", None),
            P("dp"),
            P("dp", None),
        ),
        check_vma=False,
    )
```

time: 67.3 us -> 52.3 us (0.78)
  local copies, waits for them, and re-layouts: 8.03 us -> 0 us
  Pallas kernels: 58.3 us -> 51.5 us
    pallas_call x1, Pallas kernels: 58.3 us -> 49.6 us  [body(): pl.pallas_call(functools.partial(kernel, grid, N), out_shape=(jax.ShapeDt...]
    slice x2 -> x0, local copies, waits for them, and re-layouts: 3.19 us -> none  [the longest x1 1.71 us: body(): weights[:, 0:4 * HD]]
    unnamed x11 -> x0, local copies, waits for them, and re-layouts: 3.13 us -> none
    pallas_call x0 -> x1, Pallas kernels: none -> 1.94 us  [body(): pl.pallas_call(finish, out_shape=(jax.ShapeDtypeStruct((2, N, C), F32), j...]
where the time goes in v2:
time: 52.3 us; the launch traced here: 52.1 us
  Pallas kernels  51.5 us (98%)
  between operations  0.64 us (1%)
    pallas_call x1, Pallas kernels, body(): pl.pallas_call(functools.partial(kernel, grid, N), out_shape=(jax.ShapeDt...  49.6 us
    pallas_call x1, Pallas kernels, body(): pl.pallas_call(finish, out_shape=(jax.ShapeDtypeStruct((2, N, C), F32), j...  1.94 us

profile of v2, /device:TPU:1, one launch (start us, length us, event | category | flops | bytes accessed | tf_op | source)
XLA Modules:
  0.0 52.1 jit_solution(8339027703314852088)
XLA Ops:
  0.6 49.6 %shard_map.127 = (f32[512,128]{1,0:T(8,128)}, bf16[512,128]{1,0:T(8,128)(2,1)}, bf16[2,16,8,384]{3,2,1,0:T(8,128)(2,1)}, f32[8,128]{1,0:T(8,128)}) custom-call(f32[1,4]{1,0:T(1,128)} %bitcast.9, bf16[2,256,128]{2,1,0:T(8,128)(2,1)} %pair_hbm.1, s32[1,256]{1,0:T(1,128)} %bitcast.6, s32[1,256]{1,0:T(1,128)} %bitcast.7, bf16[128,512]{1,0:T(8,128)(2,1)} %w_hbm.1, ...), custom_call_target="tpu_custom_call" | custom-call | tf_op jit(solution)/shard_map/pallas_call | solution.py:621
  50.2 1.9 %shard_map.128 = (f32[2,256,128]{2,1,0:T(8,128)}, bf16[2,256,128]{2,1,0:T(8,128)(2,1)}, f32[128,512]{1,0:T(8,128)}, f32[4,128]{1,0:T(4,128)}, f32[1,4]{1,0:T(1,128)}, /*index=5*/f32[128,128]{1,0:T(8,128)}) custom-call(f32[512,128]{1,0:T(8,128)} %get-tuple-element.16.npt_ref, bf16[512,128]{1,0:T(8,128)(2,1)} %get-tuple-element.17.pg_ref, ...), custom_call_target="tpu_custom_call" | custom-call | tf_op jit(solution)/shard_map/pallas_call | solution.py:643

commit v3 on v2

--- a/solution.py
+++ b/solution.py
@@ -48,9 +48,6 @@
     bw_ref,
     ow_ref,
     cot_ref,
-    npt_ref,
-    pg_ref,
-    small_ref,
     std_ref,
     inv_ref,
     normed_ref,
@@ -93,7 +90,6 @@
     t0_ref,
     t1_ref,
     in_s,
-    out_s,
     slot_s,
     slot_r,
     ag_s,
@@ -159,7 +155,9 @@
     steps = [(i, j) for i in range(NY) for j in range(NX) if i or j]
     steps.sort(key=lambda s: -min(s[0], NY - s[0]) - min(s[1], NX - s[1]))
     plane = [lax.rem(y + i, NY) * NX + lax.rem(x + j, NX) for i, j in steps]
-    column = others(zc, G)
+    reach = list(range(1, G))
+    reach.sort(key=lambda d: -min(d // NC, NZ - d // NC))
+    column = [lax.rem(zc - c + d - d % NC, G) + lax.rem(c + d, NC) for d in reach]
 
     def copy(src, dst, ssem, rsem, dev):
         return pltpu.make_async_remote_copy(
@@ -171,18 +169,19 @@
             device_id_type=pl.DeviceIdType.MESH,
         )
 
-    sent = []
+    drains = []
 
     def send(src, dst, ssem, rsem, dev):
-        d = copy(src, dst, ssem, rsem, dev)
-        d.start()
-        sent.append(d)
+        copy(src, dst, ssem, rsem, dev).start()
 
     def arrived(ref, sem):
         copy(ref, ref, sem, sem, partner).wait_recv()
 
+    def later(ref, sem):
+        drains.append(copy(ref, ref, sem, sem, partner))
+
     barrier = pltpu.get_barrier_semaphore()
-    peers = [yx_peer(b) for b in plane] + [zc_peer(g) for g in column]
+    peers = [zc_peer(g) for g in column] + [yx_peer(b) for b in plane]
     for p in peers:
         pl.semaphore_signal(
             barrier, inc=1, device_id={"dap": p}, device_id_type=pl.DeviceIdType.MESH
@@ -224,7 +223,8 @@
 
     pl.semaphore_wait(barrier, len(peers))
     for g in column:
-        send(slot_ref.at[zc], slot_ref.at[zc], slot_s.at[g], slot_r.at[zc], zc_peer(g))
+        send(slot_ref.at[zc], slot_ref.at[zc], slot_s, slot_r, zc_peer(g))
+    later(slot_ref.at[pl.ds(0, G - 1)], slot_s)
 
     for d in loads[2:]:
         d.wait()
@@ -245,25 +245,18 @@
         qt_ref[r] = jnp.transpose(q32[rows]).astype(BF16)
         dat_ref[r] = jnp.transpose(da32[rows]).astype(BF16)
 
-    for g in column:
-        arrived(slot_ref.at[g], slot_r.at[g])
+    arrived(slot_ref.at[pl.ds(0, G - 1)], slot_r)
     gathered = slot_ref[...].reshape(G * 2 * H, N)
     for t in range(HC):
         at = lax.broadcasted_iota(jnp.int32, (BR, G * 2 * H), 0) * H + (far + t)
         pick = (at == lax.broadcasted_iota(jnp.int32, (BR, G * 2 * H), 1)).astype(BF16)
         bias_ref[far + t, yx] = dot(pick, gathered).astype(BF16)
 
-    def bias_block(first, block):
-        return bias_ref.at[pl.ds(first, HC), block]
-
-    def hand_over(block):
-        part = bias_block(far, block)
-        send(part, part, agc_s.at[block], agc_r.at[block], partner)
-
-    for number, b in enumerate(plane):
-        part = bias_block(far, yx)
-        send(part, part, ag_s.at[number], ag_r.at[yx], yx_peer(b))
-    hand_over(yx)
+    part = bias_ref.at[pl.ds(far, HC), yx]
+    for b in plane:
+        send(part, part, ag_s, ag_r, yx_peer(b))
+    most = bias_ref.at[pl.ds(far, HC), pl.ds(0, NB - 1)]
+    later(most, ag_s)
 
     chain = chain_ref[...].astype(F32)
     chain_cols = jnp.transpose(jnp.broadcast_to(chain, (HD, N)))
@@ -285,9 +278,14 @@
             s0_ref[r, h] = products + extra
             dp_ref[r, h] = dot(jnp.where(own, da_ref[rows, :], none), v_ref[rows, :], NT)
 
-    for b in plane:
-        arrived(bias_block(far, b), ag_r.at[b])
-        hand_over(b)
+    arrived(most, ag_r)
+
+    def handed(first, t):
+        part = bias_ref.at[first + t]
+        return copy(part, part, agc_s.at[t], agc_r.at[t], partner)
+
+    for t in range(HC):
+        handed(far, t).start()
 
     att_ref[...] = jnp.zeros((2, N, HD), F32)
     dq_ref[...] = jnp.zeros((2, N, HD), F32)
@@ -324,27 +322,17 @@
         sc_ref[t] = dbias_ref[far + t].reshape(NB, BR, N).astype(BF16)
         rsc(t).start()
 
-    for b in [yx] + plane:
-        arrived(bias_block(near, b), agc_r.at[b])
-
-    def plane_copy(t, number):
-        b = plane[number]
-        return copy(
-            sa_ref.at[t, b],
-            ra_ref.at[yx, t],
-            rsa_s.at[t, number],
-            rsa_r.at[t, yx],
-            yx_peer(b),
-        )
-
     @pl.loop(0, HC)
     def _(t):
+        handed(near, t).wait_recv()
         one_head(near + t)
         rsc(t).wait_recv()
         total = dbias_ref[near + t] + rc_ref[t].reshape(N, N).astype(F32)
         sa_ref[t] = total.reshape(NB, BR, N).astype(BF16)
-        for number in range(NB - 1):
-            plane_copy(t, number).start()
+        for b in plane:
+            send(sa_ref.at[t, b], ra_ref.at[yx, t], rsa_s, rsa_r, yx_peer(b))
+
+    later(ra_ref.at[pl.ds(0, NB - 1)], rsa_s)
 
     attended = att_ref[...].reshape(T, HD)
     gating = gate_ref[...]
@@ -352,10 +340,6 @@
     update = dot(gated, ow_ref[...])
     next_pair = pair_ref[...].reshape(T, C).astype(F32) + update
     us_ref[...] = next_pair.astype(BF16).reshape(2, NB, BR, C)
-    for number, b in enumerate(plane):
-        send(us_ref.at[:, b], ub_ref.at[yx], ua_s.at[number], ua_r.at[yx], yx_peer(b))
-    ub_ref[yx] = us_ref[:, yx]
-
     d_gate = dgated_ref[...] * attended * gating * (1.0 - gating)
     dproj_ref[:, 0:HD] = (dq_ref[...].reshape(T, HD) * scaling).astype(BF16)
     for r in range(2):
@@ -380,27 +364,41 @@
         value = jnp.sum(value, axis=1, keepdims=True)
         chain_sums = jnp.where((row == H) & (lane == h), value, chain_sums)
 
+    wc.wait()
+    own_half = wfull_ref[c].astype(F32) + wrc_ref[...].astype(F32)
+    wsa_ref[...] = own_half.reshape(NB, 128 // NB, 3 * HD).astype(BF16)
+    for b in plane:
+        send(wsa_ref.at[b], wra_ref.at[yx], wa_s, wa_r, yx_peer(b))
+    later(wra_ref.at[pl.ds(0, NB - 1)], wa_s)
+    wra_ref[yx] = wsa_ref[yx]
+
+    for b in plane:
+        send(us_ref.at[:, b], ub_ref.at[yx], ua_s, ua_r, yx_peer(b))
+    later(ub_ref.at[pl.ds(0, NB - 1)], ua_s)
+    ub_ref[yx] = us_ref[:, yx]
+
     total = sa_ref[:, yx].astype(F32)
+    arrived(ra_ref.at[pl.ds(0, NB - 1)], rsa_r)
     for b in plane:
-        for t in range(HC):
-            arrived(ra_ref.at[b, t], rsa_r.at[t, b])
         total = total + ra_ref[b].astype(F32)
     for g in range(G):
         for jl in range(2):
             sz_ref[g, jl * HC : (jl + 1) * HC, :] = total[:, 2 * g + jl, :]
     for g in column:
-        send(sz_ref.at[g], rz_ref.at[zc], rsz_s.at[g], rsz_r.at[zc], zc_peer(g))
+        send(sz_ref.at[g], rz_ref.at[zc], rsz_s, rsz_r, zc_peer(g))
+    later(rz_ref.at[pl.ds(0, G - 1)], rsz_s)
     rz_ref[zc] = sz_ref[zc]
 
-    wc.wait()
-    own_half = wfull_ref[c].astype(F32) + wrc_ref[...].astype(F32)
-    wsa_ref[...] = own_half.reshape(NB, 128 // NB, 3 * HD).astype(BF16)
-    for number, b in enumerate(plane):
-        send(wsa_ref.at[b], wra_ref.at[yx], wa_s.at[number], wa_r.at[yx], yx_peer(b))
-    wra_ref[yx] = wsa_ref[yx]
-
-    for b in plane:
-        arrived(ub_ref.at[b], ua_r.at[b])
+    arrived(wra_ref.at[pl.ds(0, NB - 1)], wa_r)
+    wsum = wra_ref[0].astype(F32)
+    for b in range(1, NB):
+        wsum = wsum + wra_ref[b].astype(F32)
+    wrz_ref[z] = wsum.astype(BF16)
+    for zz in others(z, NZ):
+        send(wrz_ref.at[z], wrz_ref.at[z], wz_s, wz_r, z_peer(zz))
+    later(wrz_ref.at[pl.ds(0, NZ - 1)], wz_s)
+
+    arrived(ub_ref.at[pl.ds(0, NB - 1)], ua_r)
     ux_ref[...] = ub_ref[...].reshape(NB * 2 * BR, C).astype(F32)
     for g in range(G):
         for jl in range(2):
@@ -408,22 +406,13 @@
                 start = r * BR + 2 * g + jl
                 uz_ref[g, jl, r] = ux_ref[pl.ds(start, NB, stride=2 * BR), :].astype(BF16)
     for g in column:
-        send(uz_ref.at[g], ur_ref.at[zc], uz_s.at[g], uz_r.at[zc], zc_peer(g))
+        send(uz_ref.at[g], ur_ref.at[zc], uz_s, uz_r, zc_peer(g))
+    later(ur_ref.at[pl.ds(0, G - 1)], uz_s)
     ur_ref[zc] = uz_ref[zc]
 
     d_normed = dot(dproj_ref[...], w_ref[...], NT)
 
-    for b in plane:
-        arrived(wra_ref.at[b], wa_r.at[b])
-    wsum = wra_ref[0].astype(F32)
-    for b in range(1, NB):
-        wsum = wsum + wra_ref[b].astype(F32)
-    wrz_ref[z] = wsum.astype(BF16)
-    for number, zz in enumerate(others(z, NZ)):
-        send(wrz_ref.at[z], wrz_ref.at[z], wz_s.at[number], wz_r.at[z], z_peer(zz))
-
-    for g in column:
-        arrived(rz_ref.at[g], rsz_r.at[g])
+    arrived(rz_ref.at[pl.ds(0, G - 1)], rsz_r)
     sums = []
     for core in range(NC):
         part = rz_ref[core]
@@ -440,77 +429,63 @@
 
     t0_ref[zc] = dot(d_bias, normed_ref[...]) + chain_sums
     for g in column:
-        send(t0_ref.at[zc], t0_ref.at[zc], t0_s.at[g], t0_r.at[zc], zc_peer(g))
+        send(t0_ref.at[zc], t0_ref.at[zc], t0_s, t0_r, zc_peer(g))
+    later(t0_ref.at[pl.ds(0, G - 1)], t0_s)
 
     d_normed = d_normed + dot(d_bias, bwt, TN)
     standard = std_ref[...]
     mean_grad = jnp.mean(d_normed, axis=-1, keepdims=True)
     mean_cross = jnp.mean(d_normed * standard, axis=-1, keepdims=True)
     pair_grad = (d_normed - mean_grad - standard * mean_cross) * inv_ref[...]
-    pg_ref[...] = pair_grad.astype(BF16)
-    pg_out = pltpu.make_async_copy(pg_ref, pg_o, out_s.at[0])
-    pg_out.start()
-
-    for g in column:
-        arrived(ur_ref.at[g], uz_r.at[g])
+    pg_o[...] = pair_grad.astype(BF16)
+
+    arrived(wrz_ref.at[pl.ds(0, NZ - 1)], wz_r)
+    wsum = wrz_ref[0].astype(F32)
+    for zz in range(1, NZ):
+        wsum = wsum + wrz_ref[zz].astype(F32)
+    wag_ref[c, yx] = wsum.astype(BF16)
+
+    part = wag_ref.at[c, yx]
+    for b in plane:
+        send(part, part, wga_s, wga_r, yx_peer(b))
+    most = wag_ref.at[c, pl.ds(0, NB - 1)]
+    later(most, wga_s)
+
+    arrived(t0_ref.at[pl.ds(0, G - 1)], t0_r)
+    small = t0_ref[0]
+    for g in range(1, G):
+        small = small + t0_ref[g]
+    t1_ref[yx] = small
+    for b in plane:
+        send(t1_ref.at[yx], t1_ref.at[yx], t1_s, t1_r, yx_peer(b))
+    later(t1_ref.at[pl.ds(0, NB - 1)], t1_s)
+
+    arrived(ur_ref.at[pl.ds(0, G - 1)], uz_r)
     for g in range(G):
         for jl in range(2):
             for r in range(2):
                 start = jl * N + 2 * g + r
-                npt_ref[pl.ds(start, NB, stride=BR), :] = ur_ref[g, jl, r].astype(F32)
-    npt_out = pltpu.make_async_copy(npt_ref, npt_o, out_s.at[1])
-    npt_out.start()
-
-    for zz in others(z, NZ):
-        arrived(wrz_ref.at[zz], wz_r.at[zz])
-    wsum = wrz_ref[0].astype(F32)
-    for zz in range(1, NZ):
-        wsum = wsum + wrz_ref[zz].astype(F32)
-    wag_ref[c, yx] = wsum.astype(BF16)
-
-    def pass_on(b):
-        part = wag_ref.at[c, b]
-        send(part, part, wgc_s.at[b], wgc_r.at[b], partner)
-
-    for number, b in enumerate(plane):
-        part = wag_ref.at[c, yx]
-        send(part, part, wga_s.at[number], wga_r.at[yx], yx_peer(b))
-    pass_on(yx)
-
-    for g in column:
-        arrived(t0_ref.at[g], t0_r.at[g])
-    small = t0_ref[0]
-    for g in range(1, G):
-        small = small + t0_ref[g]
-    t1_ref[yx] = small
-    for number, b in enumerate(plane):
-        send(t1_ref.at[yx], t1_ref.at[yx], t1_s.at[number], t1_r.at[yx], yx_peer(b))
-
-    for b in plane:
-        arrived(wag_ref.at[c, b], wga_r.at[b])
-        pass_on(b)
-    for b in [yx] + plane:
-        arrived(wag_ref.at[1 - c, b], wgc_r.at[b])
-    wag_out = pltpu.make_async_copy(wag_ref, wag_o, out_s.at[2])
-    wag_out.start()
-
-    for b in plane:
-        arrived(t1_ref.at[b], t1_r.at[b])
+                npt_o[pl.ds(start, NB, stride=BR), :] = ur_ref[g, jl, r].astype(F32)
+
+    arrived(most, wga_r)
+    part = wag_ref.at[c]
+    wgc = copy(part, part, wgc_s, wgc_r, partner)
+    wgc.start()
+
+    arrived(t1_ref.at[pl.ds(0, NB - 1)], t1_r)
     small = t1_ref[0]
     for b in range(1, NB):
         small = small + t1_ref[b]
-    small_ref[...] = small * (1.0 / N)
-    small_out = pltpu.make_async_copy(small_ref, small_o, out_s.at[3])
-    small_out.start()
-
-    for d in sent:
+    small_o[...] = small * (1.0 / N)
+    wgc.wait_recv()
+    wag_o[...] = wag_ref[...]
+
+    wgc.wait_send()
+    for d in drains:
         d.wait_send()
     for t in range(HC):
         rsc(t).wait_send()
-        for number in range(NB - 1):
-            plane_copy(t, number).wait_send()
-    for d in (pg_out, npt_out, wag_out, small_out):
-        d.wait()
+        handed(far, t).wait_send()
 
 
 def scratch(grid, N):
@@ -527,9 +502,6 @@
         V((H, C), BF16),
         V((HD, C), BF16),
         V((2, N, C), BF16),
-        V((T, C), F32),
-        V((T, C), BF16),
-        V((8, C), F32),
         V((T, C), F32),
         V((T, C), F32),
         V((T, C), BF16),
@@ -573,27 +545,11 @@
         V((NB, 8, C), F32),
     ]
     dma = pltpu.SemaphoreType.DMA
-    counts = [
-        ((8,), (4,)),
-        ((G,), (G,)),
-        ((NB,), (NB,)),
-        ((NB,), (NB,)),
-        ((HC,), (HC,)),
-        ((HC, NB), (HC, NB)),
-        ((G,), (G,)),
-        (None, None),
-        ((NB,), (NB,)),
-        ((NZ,), (NZ,)),
-        ((NB,), (NB,)),
-        ((NB,), (NB,)),
-        ((NB,), (NB,)),
-        ((G,), (G,)),
-        ((G,), (G,)),
-        ((NB,), (NB,)),
-    ]
-    for both in counts:
-        for shape in both:
-            buffers.append(dma if shape is None else dma(shape))
+    pairs = [None] * 16
+    pairs[3] = pairs[4] = (HC,)
+    buffers.append(dma((8,)))
+    for shape in pairs[1:]:
+        buffers += [dma if shape is None else dma(shape)] * 2
     return buffers
 
 
@@ -621,13 +577,13 @@
     results = pl.pallas_call(
         functools.partial(kernel, grid, N),
         out_shape=(
-            jax.ShapeDtypeStruct((2 * N, C), F32),
-            jax.ShapeDtypeStruct((2 * N, C), BF16),
-            jax.ShapeDtypeStruct((NC, NX * NY, 128 // (NX * NY), 3 * HD), BF16),
-            jax.ShapeDtypeStruct((8, C), F32),
+            pltpu.VMEM((2 * N, C), F32),
+            pltpu.VMEM((2 * N, C), BF16),
+            pltpu.VMEM((NC, NX * NY, 128 // (NX * NY), 3 * HD), BF16),
+            pltpu.VMEM((8, C), F32),
         ),
         in_specs=[hbm] * 8,
-        out_specs=(hbm,) * 4,
+        out_specs=(vmem,) * 4,
         scratch_shapes=scratch(grid, N),
         compiler_params=pltpu.CompilerParams(collective_id=0, has_side_effects=True),
     )(
@@ -652,7 +608,7 @@
         ),
         in_specs=[vmem] * 4,
         out_specs=(vmem,) * 6,
-    )(*results)
+    )(*[pltpu.with_memory_space_constraint(r, pltpu.VMEM) for r in results])
     return (
         npt,
         pair_grad,

time: 52.3 us -> 45.2 us (0.86)
  Pallas kernels: 51.5 us -> 44.5 us
    pallas_call x1, Pallas kernels: 49.6 us -> 43.6 us  [body(): pl.pallas_call(functools.partial(kernel, grid, N), out_shape=(pltpu.VMEM(...]
    pallas_call x1, Pallas kernels: 1.94 us -> 0.89 us  [body(): pl.pallas_call(finish, out_shape=(jax.ShapeDtypeStruct((2, N, C), F32), j...]
where the time goes in v3:
time: 45.2 us; the launch traced here: 45.1 us
  Pallas kernels  44.5 us (98%)
  between operations  0.64 us (1%)
    pallas_call x1, Pallas kernels, body(): pl.pallas_call(functools.partial(kernel, grid, N), out_shape=(pltpu.VMEM(...  43.6 us

profile of v3, /device:TPU:1, one launch (start us, length us, event | category | flops | bytes accessed | tf_op | source)
XLA Modules:
  0.0 45.1 jit_solution(6558482661602037106)
XLA Ops:
  0.6 43.6 %shard_map.127 = (f32[512,128]{1,0:T(8,128)S(1)}, bf16[512,128]{1,0:T(8,128)(2,1)S(1)}, bf16[2,16,8,384]{3,2,1,0:T(8,128)(2,1)S(1)}, f32[8,128]{1,0:T(8,128)S(1)}) custom-call(f32[1,4]{1,0:T(1,128)} %bitcast.9, bf16[2,256,128]{2,1,0:T(8,128)(2,1)} %pair_hbm.1, s32[1,256]{1,0:T(1,128)} %bitcast.6, s32[1,256]{1,0:T(1,128)} %bitcast.7, bf16[128,512]{1,0:T(8,128)(2,1)} %w_hbm.1, ...), custom_call_target="tpu_custom_call" | custom-call | tf_op jit(solution)/shard_map/pallas_call | solution.py:577
  44.3 0.9 %shard_map.128 = (f32[2,256,128]{2,1,0:T(8,128)}, bf16[2,256,128]{2,1,0:T(8,128)(2,1)}, f32[128,512]{1,0:T(8,128)}, f32[4,128]{1,0:T(4,128)}, f32[1,4]{1,0:T(1,128)}, /*index=5*/f32[128,128]{1,0:T(8,128)}) custom-call(f32[512,128]{1,0:T(8,128)S(1)} %get-tuple-element.16.npt_ref, bf16[512,128]{1,0:T(8,128)(2,1)S(1)} %get-tuple-element.17.pg_ref, ...), custom_call_target="tpu_custom_call" | custom-call | tf_op jit(solution)/shard_map/pallas_call | solution.py:599

commit v4 on v3

--- a/solution.py
+++ b/solution.py
@@ -89,6 +89,7 @@
     ur_ref,
     t0_ref,
     t1_ref,
+    rows_ref,
     in_s,
     slot_s,
     slot_r,
@@ -120,6 +121,10 @@
     t0_r,
     t1_s,
     t1_r,
+    nz_s,
+    nz_r,
+    nc_s,
+    nc_r,
 ):
     NY, NX, NZ, NC = grid
     G = NZ * NC
@@ -213,6 +218,7 @@
     inv_ref[...] = jnp.broadcast_to(inverse, (T, C))
     normed = standard.astype(BF16)
     normed_ref[...] = normed
+    rows_ref[z, c] = normed
     loads[1].wait()
     bwt = jnp.concatenate([bw_ref[...].astype(F32), jnp.zeros((8 - H, C), F32)], axis=0)
     bwt = bwt.astype(BF16)
@@ -245,19 +251,6 @@
         qt_ref[r] = jnp.transpose(q32[rows]).astype(BF16)
         dat_ref[r] = jnp.transpose(da32[rows]).astype(BF16)
 
-    arrived(slot_ref.at[pl.ds(0, G - 1)], slot_r)
-    gathered = slot_ref[...].reshape(G * 2 * H, N)
-    for t in range(HC):
-        at = lax.broadcasted_iota(jnp.int32, (BR, G * 2 * H), 0) * H + (far + t)
-        pick = (at == lax.broadcasted_iota(jnp.int32, (BR, G * 2 * H), 1)).astype(BF16)
-        bias_ref[far + t, yx] = dot(pick, gathered).astype(BF16)
-
-    part = bias_ref.at[pl.ds(far, HC), yx]
-    for b in plane:
-        send(part, part, ag_s, ag_r, yx_peer(b))
-    most = bias_ref.at[pl.ds(far, HC), pl.ds(0, NB - 1)]
-    later(most, ag_s)
-
     chain = chain_ref[...].astype(F32)
     chain_cols = jnp.transpose(jnp.broadcast_to(chain, (HD, N)))
     chain_cols = jnp.concatenate([chain_cols] * (-(-N // HD)), axis=1)[:, 0:N]
@@ -277,6 +270,31 @@
             products = dot(jnp.where(own, q_ref[rows, :], none), k_ref[rows, :], NT)
             s0_ref[r, h] = products + extra
             dp_ref[r, h] = dot(jnp.where(own, da_ref[rows, :], none), v_ref[rows, :], NT)
+
+    part = rows_ref.at[z, c]
+    round_z = [lax.rem(z + d, NZ) for d in ((2, 1, 3) if NZ == 4 else range(1, NZ))]
+    for number, zz in enumerate(round_z):
+        send(part, part, nz_s, nz_r.at[number], z_peer(zz))
+    later(rows_ref.at[pl.ds(0, NZ - 1), c], nz_s)
+
+    def row_slot(zz):
+        part = rows_ref.at[zz, c]
+        send(part, part, nc_s, nc_r, partner)
+
+    row_slot(z)
+
+    arrived(slot_ref.at[pl.ds(0, G - 1)], slot_r)
+    gathered = slot_ref[...].reshape(G * 2 * H, N)
+    for t in range(HC):
+        at = lax.broadcasted_iota(jnp.int32, (BR, G * 2 * H), 0) * H + (far + t)
+        pick = (at == lax.broadcasted_iota(jnp.int32, (BR, G * 2 * H), 1)).astype(BF16)
+        bias_ref[far + t, yx] = dot(pick, gathered).astype(BF16)
+
+    part = bias_ref.at[pl.ds(far, HC), yx]
+    for b in plane:
+        send(part, part, ag_s, ag_r, yx_peer(b))
+    most = bias_ref.at[pl.ds(far, HC), pl.ds(0, NB - 1)]
+    later(most, ag_s)
 
     arrived(most, ag_r)
 
@@ -377,6 +395,12 @@
     later(ub_ref.at[pl.ds(0, NB - 1)], ua_s)
     ub_ref[yx] = us_ref[:, yx]
 
+    for number, d in enumerate((2, 3, 1) if NZ == 4 else range(NZ - 1, 0, -1)):
+        zz = lax.rem(z + d, NZ)
+        arrived(rows_ref.at[zz, c], nz_r.at[number])
+        row_slot(zz)
+    later(rows_ref.at[:, c], nc_s)
+
     total = sa_ref[:, yx].astype(F32)
     arrived(ra_ref.at[pl.ds(0, NB - 1)], rsa_r)
     for b in plane:
@@ -384,10 +408,18 @@
     for g in range(G):
         for jl in range(2):
             sz_ref[g, jl * HC : (jl + 1) * HC, :] = total[:, 2 * g + jl, :]
+
+    wide = jnp.concatenate([total[:, i, :] for i in range(BR)], axis=1)
+    row = lax.broadcasted_iota(jnp.int32, (8, BR * N), 0)
+    parts = jnp.zeros((8, BR * N), F32)
+    for t in range(HC):
+        parts = jnp.where(row == near + t, wide[t : t + 1], parts)
+    arrived(rows_ref.at[:, 1 - c], nc_r)
+    small = dot(parts.astype(BF16), rows_ref[...].reshape(BR * N, C))
+    t0_ref[zc] = small + chain_sums
     for g in column:
-        send(sz_ref.at[g], rz_ref.at[zc], rsz_s, rsz_r, zc_peer(g))
-    later(rz_ref.at[pl.ds(0, G - 1)], rsz_s)
-    rz_ref[zc] = sz_ref[zc]
+        send(t0_ref.at[zc], t0_ref.at[zc], t0_s, t0_r, zc_peer(g))
+    later(t0_ref.at[pl.ds(0, G - 1)], t0_s)
 
     arrived(wra_ref.at[pl.ds(0, NB - 1)], wa_r)
     wsum = wra_ref[0].astype(F32)
@@ -397,6 +429,11 @@
     for zz in others(z, NZ):
         send(wrz_ref.at[z], wrz_ref.at[z], wz_s, wz_r, z_peer(zz))
     later(wrz_ref.at[pl.ds(0, NZ - 1)], wz_s)
+
+    for g in column:
+        send(sz_ref.at[g], rz_ref.at[zc], rsz_s, rsz_r, zc_peer(g))
+    later(rz_ref.at[pl.ds(0, G - 1)], rsz_s)
+    rz_ref[zc] = sz_ref[zc]
 
     arrived(ub_ref.at[pl.ds(0, NB - 1)], ua_r)
     ux_ref[...] = ub_ref[...].reshape(NB * 2 * BR, C).astype(F32)
@@ -411,6 +448,27 @@
     ur_ref[zc] = uz_ref[zc]
 
     d_normed = dot(dproj_ref[...], w_ref[...], NT)
+
+    arrived(t0_ref.at[pl.ds(0, G - 1)], t0_r)
+    small = t0_ref[0]
+    for g in range(1, G):
+        small = small + t0_ref[g]
+    t1_ref[yx] = small
+    for b in plane:
+        send(t1_ref.at[yx], t1_ref.at[yx], t1_s, t1_r, yx_peer(b))
+    later(t1_ref.at[pl.ds(0, NB - 1)], t1_s)
+
+    arrived(wrz_ref.at[pl.ds(0, NZ - 1)], wz_r)
+    wsum = wrz_ref[0].astype(F32)
+    for zz in range(1, NZ):
+        wsum = wsum + wrz_ref[zz].astype(F32)
+    wag_ref[c, yx] = wsum.astype(BF16)
+
+    part = wag_ref.at[c, yx]
+    for b in plane:
+        send(part, part, wga_s, wga_r, yx_peer(b))
+    most = wag_ref.at[c, pl.ds(0, NB - 1)]
+    later(most, wga_s)
 
     arrived(rz_ref.at[pl.ds(0, G - 1)], rsz_r)
     sums = []
@@ -427,11 +485,6 @@
     d_bias = jnp.concatenate(d_bias, axis=1)
     d_bias = jnp.concatenate([d_bias, jnp.zeros((8 - H, T), F32)], axis=0).astype(BF16)
 
-    t0_ref[zc] = dot(d_bias, normed_ref[...]) + chain_sums
-    for g in column:
-        send(t0_ref.at[zc], t0_ref.at[zc], t0_s, t0_r, zc_peer(g))
-    later(t0_ref.at[pl.ds(0, G - 1)], t0_s)
-
     d_normed = d_normed + dot(d_bias, bwt, TN)
     standard = std_ref[...]
     mean_grad = jnp.mean(d_normed, axis=-1, keepdims=True)
@@ -439,26 +492,10 @@
     pair_grad = (d_normed - mean_grad - standard * mean_cross) * inv_ref[...]
     pg_o[...] = pair_grad.astype(BF16)
 
-    arrived(wrz_ref.at[pl.ds(0, NZ - 1)], wz_r)
-    wsum = wrz_ref[0].astype(F32)
-    for zz in range(1, NZ):
-        wsum = wsum + wrz_ref[zz].astype(F32)
-    wag_ref[c, yx] = wsum.astype(BF16)
-
-    part = wag_ref.at[c, yx]
-    for b in plane:
-        send(part, part, wga_s, wga_r, yx_peer(b))
-    most = wag_ref.at[c, pl.ds(0, NB - 1)]
-    later(most, wga_s)
-
-    arrived(t0_ref.at[pl.ds(0, G - 1)], t0_r)
-    small = t0_ref[0]
-    for g in range(1, G):
-        small = small + t0_ref[g]
-    t1_ref[yx] = small
-    for b in plane:
-        send(t1_ref.at[yx], t1_ref.at[yx], t1_s, t1_r, yx_peer(b))
-    later(t1_ref.at[pl.ds(0, NB - 1)], t1_s)
+    arrived(most, wga_r)
+    part = wag_ref.at[c]
+    wgc = copy(part, part, wgc_s, wgc_r, partner)
+    wgc.start()
 
     arrived(ur_ref.at[pl.ds(0, G - 1)], uz_r)
     for g in range(G):
@@ -466,11 +503,6 @@
             for r in range(2):
                 start = jl * N + 2 * g + r
                 npt_o[pl.ds(start, NB, stride=BR), :] = ur_ref[g, jl, r].astype(F32)
-
-    arrived(most, wga_r)
-    part = wag_ref.at[c]
-    wgc = copy(part, part, wgc_s, wgc_r, partner)
-    wgc.start()
 
     arrived(t1_ref.at[pl.ds(0, NB - 1)], t1_r)
     small = t1_ref[0]
@@ -543,13 +575,15 @@
         V((G, 2, 2, NB, C), BF16),
         V((G, 8, C), F32),
         V((NB, 8, C), F32),
+        V((NZ, NC, T, C), BF16),
     ]
     dma = pltpu.SemaphoreType.DMA
     pairs = [None] * 16
     pairs[3] = pairs[4] = (HC,)
     buffers.append(dma((8,)))
-    for shape in pairs[1:]:
+    for shape in pairs[1:16]:
         buffers += [dma if shape is None else dma(shape)] * 2
+    buffers += [dma, dma((NZ,)), dma, dma]
     return buffers
 
 

time: 45.2 us -> 44.2 us (0.978)
  Pallas kernels: 44.5 us -> 43.5 us
    pallas_call x1, Pallas kernels: 43.6 us -> 42.6 us  [body(): pl.pallas_call(functools.partial(kernel, grid, N), out_shape=(pltpu.VMEM(...]
where the time goes in v4:
time: 44.2 us; the launch traced here: 44.1 us
  Pallas kernels  43.5 us (98%)
  between operations  0.64 us (1%)
    pallas_call x1, Pallas kernels, body(): pl.pallas_call(functools.partial(kernel, grid, N), out_shape=(pltpu.VMEM(...  42.6 us
    pallas_call x1, Pallas kernels, body(): pl.pallas_call(finish, out_shape=(jax.ShapeDtypeStruct((2, N, C), F32), j...  0.89 us

profile of v4, /device:TPU:1, one launch (start us, length us, event | category | flops | bytes accessed | tf_op | source)
XLA Modules:
  0.0 44.1 jit_solution(11620056939244163775)
XLA Ops:
  0.6 42.6 %shard_map.127 = (f32[512,128]{1,0:T(8,128)S(1)}, bf16[512,128]{1,0:T(8,128)(2,1)S(1)}, bf16[2,16,8,384]{3,2,1,0:T(8,128)(2,1)S(1)}, f32[8,128]{1,0:T(8,128)S(1)}) custom-call(f32[1,4]{1,0:T(1,128)} %bitcast.9, bf16[2,256,128]{2,1,0:T(8,128)(2,1)} %pair_hbm.1, s32[1,256]{1,0:T(1,128)} %bitcast.6, s32[1,256]{1,0:T(1,128)} %bitcast.7, bf16[128,512]{1,0:T(8,128)(2,1)} %w_hbm.1, ...), custom_call_target="tpu_custom_call" | custom-call | tf_op jit(solution)/shard_map/pallas_call | solution.py:611
  43.2 0.9 %shard_map.128 = (f32[2,256,128]{2,1,0:T(8,128)}, bf16[2,256,128]{2,1,0:T(8,128)(2,1)}, f32[128,512]{1,0:T(8,128)}, f32[4,128]{1,0:T(4,128)}, f32[1,4]{1,0:T(1,128)}, /*index=5*/f32[128,128]{1,0:T(8,128)}) custom-call(f32[512,128]{1,0:T(8,128)S(1)} %get-tuple-element.16.npt_ref, bf16[512,128]{1,0:T(8,128)(2,1)S(1)} %get-tuple-element.17.pg_ref, ...), custom_call_target="tpu_custom_call" | custom-call | tf_op jit(solution)/shard_map/pallas_call | solution.py:633

commit v5 on v4

--- a/solution.py
+++ b/solution.py
@@ -50,7 +50,6 @@
     cot_ref,
     std_ref,
     inv_ref,
-    normed_ref,
     q_ref,
     k_ref,
     v_ref,
@@ -61,8 +60,7 @@
     dgated_ref,
     att_ref,
     dq_ref,
-    dkt_ref,
-    dvt_ref,
+    dkv_ref,
     same_ref,
     dbias_ref,
     dproj_ref,
@@ -70,14 +68,10 @@
     dp_ref,
     slot_ref,
     bias_ref,
-    sc_ref,
-    rc_ref,
     sa_ref,
     ra_ref,
     sz_ref,
     rz_ref,
-    wfull_ref,
-    wrc_ref,
     wsa_ref,
     wra_ref,
     wrz_ref,
@@ -90,21 +84,22 @@
     t0_ref,
     t1_ref,
     rows_ref,
+    u32_ref,
+    u16_ref,
+    up_ref,
+    d16_ref,
+    dn_ref,
+    wc_ref,
+    outp_ref,
     in_s,
     slot_s,
     slot_r,
     ag_s,
     ag_r,
-    agc_s,
-    agc_r,
-    rsc_s,
-    rsc_r,
     rsa_s,
     rsa_r,
     rsz_s,
     rsz_r,
-    wc_s,
-    wc_r,
     wa_s,
     wa_r,
     wz_s,
@@ -121,6 +116,14 @@
     t0_r,
     t1_s,
     t1_r,
+    pn_s,
+    pn_r,
+    pc_s,
+    pc_r,
+    up_s,
+    up_r,
+    dn_s,
+    dn_r,
     nz_s,
     nz_r,
     nc_s,
@@ -142,8 +145,8 @@
     x = lax.rem(yx, NX)
     y = lax.div(yx, NX)
     partner = idx + 1 - 2 * c
-    far = HC * (1 - c)
     near = HC * c
+    HW = HC * DH
 
     def zc_peer(g):
         return idx + g - zc
@@ -198,7 +201,7 @@
             (pair_hbm, pair_ref),
             (bw_hbm, bw_ref),
             (w_hbm, w_ref),
-            (cot_hbm, cot_ref),
+            (cot_hbm, cot_ref.at[c]),
             (ow_hbm, ow_ref),
             (chain_hbm, chain_ref),
             (mask_hbm, mask_ref),
@@ -217,7 +220,6 @@
     std_ref[...] = standard
     inv_ref[...] = jnp.broadcast_to(inverse, (T, C))
     normed = standard.astype(BF16)
-    normed_ref[...] = normed
     rows_ref[z, c] = normed
     loads[1].wait()
     bwt = jnp.concatenate([bw_ref[...].astype(F32), jnp.zeros((8 - H, C), F32)], axis=0)
@@ -231,25 +233,47 @@
     for g in column:
         send(slot_ref.at[zc], slot_ref.at[zc], slot_s, slot_r, zc_peer(g))
     later(slot_ref.at[pl.ds(0, G - 1)], slot_s)
-
+    part = rows_ref.at[z, c]
+    send(part, part, pn_s, pn_r, partner)
+    later(part, pn_s)
     for d in loads[2:]:
         d.wait()
-    projected = dot(normed, w_ref[...])
+    send(cot_ref.at[c], cot_ref.at[c], pc_s, pc_r, partner)
+    later(cot_ref.at[c], pc_s)
+
     scaling = DH ** (-0.5)
-    q32 = projected[:, 0:HD] * scaling
-    q_ref[...] = q32.astype(BF16)
-    k_ref[...] = projected[:, HD : 2 * HD].astype(BF16)
-    v_ref[...] = projected[:, 2 * HD : 3 * HD].astype(BF16)
-    gating = jax.nn.sigmoid(projected[:, 3 * HD :])
-    gate_ref[...] = gating
-    d_gated = dot(cot_ref[...].reshape(T, C), ow_ref[...], NT)
-    dgated_ref[...] = d_gated
-    da32 = d_gated * gating
-    da_ref[...] = da32.astype(BF16)
-    for r in range(2):
-        rows = slice(r * N, (r + 1) * N)
-        qt_ref[r] = jnp.transpose(q32[rows]).astype(BF16)
-        dat_ref[r] = jnp.transpose(da32[rows]).astype(BF16)
+
+    def project(core):
+        projected = dot(rows_ref[z, core], w_ref[...])
+        q32 = projected[:, 0:HD] * scaling
+        q_ref[core] = q32.astype(BF16)
+        k_ref[core] = projected[:, HD : 2 * HD].astype(BF16)
+        v_ref[core] = projected[:, 2 * HD : 3 * HD].astype(BF16)
+        gating = jax.nn.sigmoid(projected[:, 3 * HD :])
+        gate_ref[core] = gating
+        d_gated = dot(cot_ref[core].reshape(T, C), ow_ref[...], NT)
+        dgated_ref[core] = d_gated
+        da32 = d_gated * gating
+        da_ref[core] = da32.astype(BF16)
+        for r in range(2):
+            rows = slice(r * N, (r + 1) * N)
+            qt_ref[core, r] = jnp.transpose(q32[rows]).astype(BF16)
+            dat_ref[core, r] = jnp.transpose(da32[rows]).astype(BF16)
+
+    project(c)
+    arrived(rows_ref.at[z, 1 - c], pn_r)
+    arrived(cot_ref.at[1 - c], pc_r)
+    project(1 - c)
+
+    part = rows_ref.at[z, c]
+    round_z = [lax.rem(z + d, NZ) for d in ((2, 1, 3) if NZ == 4 else range(1, NZ))]
+    for number, zz in enumerate(round_z):
+        send(part, part, nz_s, nz_r.at[number], z_peer(zz))
+    later(rows_ref.at[pl.ds(0, NZ - 1), c], nz_s)
+
+    def row_slot(zz):
+        part = rows_ref.at[zz, c]
+        send(part, part, nc_s, nc_r, partner)
 
     chain = chain_ref[...].astype(F32)
     chain_cols = jnp.transpose(jnp.broadcast_to(chain, (HD, N)))
@@ -259,137 +283,117 @@
     head_of = lax.broadcasted_iota(jnp.int32, (N, HD), 1) // DH
     none = jnp.zeros((N, HD), BF16)
 
-    @pl.loop(0, H)
-    def _(h):
+    @pl.loop(0, HC)
+    def _(t):
+        h = near + t
         own = head_of == h
         lane = lax.broadcasted_iota(jnp.int32, (1, H), 1) == h
         weight = jnp.sum(jnp.where(lane, cw_ref[...], 0.0), axis=1, keepdims=True)
         extra = weight * same_ref[...] + masked
-        for r in range(2):
-            rows = slice(r * N, (r + 1) * N)
-            products = dot(jnp.where(own, q_ref[rows, :], none), k_ref[rows, :], NT)
-            s0_ref[r, h] = products + extra
-            dp_ref[r, h] = dot(jnp.where(own, da_ref[rows, :], none), v_ref[rows, :], NT)
-
-    part = rows_ref.at[z, c]
-    round_z = [lax.rem(z + d, NZ) for d in ((2, 1, 3) if NZ == 4 else range(1, NZ))]
-    for number, zz in enumerate(round_z):
-        send(part, part, nz_s, nz_r.at[number], z_peer(zz))
-    later(rows_ref.at[pl.ds(0, NZ - 1), c], nz_s)
-
-    def row_slot(zz):
-        part = rows_ref.at[zz, c]
-        send(part, part, nc_s, nc_r, partner)
-
-    row_slot(z)
+        for core in range(NC):
+            for r in range(2):
+                rows = slice(r * N, (r + 1) * N)
+                query = jnp.where(own, q_ref[core, rows, :], none)
+                s0_ref[t, core, r] = dot(query, k_ref[core, rows, :], NT) + extra
+                grad = jnp.where(own, da_ref[core, rows, :], none)
+                dp_ref[t, core, r] = dot(grad, v_ref[core, rows, :], NT)
 
     arrived(slot_ref.at[pl.ds(0, G - 1)], slot_r)
     gathered = slot_ref[...].reshape(G * 2 * H, N)
     for t in range(HC):
-        at = lax.broadcasted_iota(jnp.int32, (BR, G * 2 * H), 0) * H + (far + t)
+        at = lax.broadcasted_iota(jnp.int32, (BR, G * 2 * H), 0) * H + (near + t)
         pick = (at == lax.broadcasted_iota(jnp.int32, (BR, G * 2 * H), 1)).astype(BF16)
-        bias_ref[far + t, yx] = dot(pick, gathered).astype(BF16)
-
-    part = bias_ref.at[pl.ds(far, HC), yx]
+        bias_ref[t, yx] = dot(pick, gathered).astype(BF16)
+
     for b in plane:
-        send(part, part, ag_s, ag_r, yx_peer(b))
-    most = bias_ref.at[pl.ds(far, HC), pl.ds(0, NB - 1)]
+        send(bias_ref.at[:, yx], bias_ref.at[:, yx], ag_s, ag_r, yx_peer(b))
+    most = bias_ref.at[:, pl.ds(0, NB - 1)]
     later(most, ag_s)
 
     arrived(most, ag_r)
 
-    def handed(first, t):
-        part = bias_ref.at[first + t]
-        return copy(part, part, agc_s.at[t], agc_r.at[t], partner)
-
-    for t in range(HC):
-        handed(far, t).start()
-
-    att_ref[...] = jnp.zeros((2, N, HD), F32)
-    dq_ref[...] = jnp.zeros((2, N, HD), F32)
-
-    def one_head(h):
-        own = head_of == h
-        bias = bias_ref[h].reshape(N, N).astype(F32)
-        head_rows = pl.ds(pl.multiple_of(h * DH, DH), DH)
-        for r in range(2):
-            rows = slice(r * N, (r + 1) * N)
-            scores = s0_ref[r, h] + bias
-            expo = jnp.exp(scores - jnp.max(scores, axis=1, keepdims=True))
-            probs = expo * (1.0 / jnp.sum(expo, axis=1, keepdims=True))
-            probs_low = probs.astype(BF16)
-            att_ref[r] += dot(probs_low, jnp.where(own, v_ref[rows, :], none))
-            d_probs = dp_ref[r, h]
-            inner = jnp.sum(probs * d_probs, axis=1, keepdims=True)
-            d_scores = probs * (d_probs - inner)
-            low = d_scores.astype(BF16)
-            dq_ref[r] += dot(low, jnp.where(own, k_ref[rows, :], none))
-            dkt_ref[r, head_rows, :] = dot(qt_ref[r, head_rows, :], low)
-            dvt_ref[r, head_rows, :] = dot(dat_ref[r, head_rows, :], probs_low)
-            if r == 0:
-                dbias_ref[h] = d_scores
-            else:
-                dbias_ref[h] += d_scores
-
-    def rsc(t):
-        return copy(sc_ref.at[t], rc_ref.at[t], rsc_s.at[t], rsc_r.at[t], partner)
+    att_ref[...] = jnp.zeros((NC, 2, N, HD), F32)
+    dq_ref[...] = jnp.zeros((NC, 2, N, HD), F32)
 
     @pl.loop(0, HC)
     def _(t):
-        one_head(far + t)
-        sc_ref[t] = dbias_ref[far + t].reshape(NB, BR, N).astype(BF16)
-        rsc(t).start()
-
-    @pl.loop(0, HC)
-    def _(t):
-        handed(near, t).wait_recv()
-        one_head(near + t)
-        rsc(t).wait_recv()
-        total = dbias_ref[near + t] + rc_ref[t].reshape(N, N).astype(F32)
-        sa_ref[t] = total.reshape(NB, BR, N).astype(BF16)
+        h = near + t
+        own = head_of == h
+        bias = bias_ref[t].reshape(N, N).astype(F32)
+        head_rows = pl.ds(pl.multiple_of(h * DH, DH), DH)
+        key_rows = pl.ds(pl.multiple_of(t * DH, DH), DH)
+        value_rows = pl.ds(pl.multiple_of(HW + t * DH, DH), DH)
+        for core in range(NC):
+            for r in range(2):
+                rows = slice(r * N, (r + 1) * N)
+                scores = s0_ref[t, core, r] + bias
+                expo = jnp.exp(scores - jnp.max(scores, axis=1, keepdims=True))
+                probs = expo * (1.0 / jnp.sum(expo, axis=1, keepdims=True))
+                probs_low = probs.astype(BF16)
+                values = jnp.where(own, v_ref[core, rows, :], none)
+                att_ref[core, r] += dot(probs_low, values)
+                d_probs = dp_ref[t, core, r]
+                inner = jnp.sum(probs * d_probs, axis=1, keepdims=True)
+                d_scores = probs * (d_probs - inner)
+                low = d_scores.astype(BF16)
+                dq_ref[core, r] += dot(low, jnp.where(own, k_ref[core, rows, :], none))
+                dkv_ref[core, r, key_rows, :] = dot(qt_ref[core, r, head_rows, :], low)
+                dkv_ref[core, r, value_rows, :] = dot(
+                    dat_ref[core, r, head_rows, :], probs_low
+                )
+                if core == 0 and r == 0:
+                    dbias_ref[t] = d_scores
+                else:
+                    dbias_ref[t] += d_scores
+        sa_ref[t] = dbias_ref[t].reshape(NB, BR, N).astype(BF16)
         for b in plane:
             send(sa_ref.at[t, b], ra_ref.at[yx, t], rsa_s, rsa_r, yx_peer(b))
 
     later(ra_ref.at[pl.ds(0, NB - 1)], rsa_s)
 
-    attended = att_ref[...].reshape(T, HD)
-    gating = gate_ref[...]
+    rows_all = NC * T
+    attended = att_ref[...].reshape(rows_all, HD)
+    gating = gate_ref[...].reshape(rows_all, HD)
     gated = (gating * attended).astype(BF16)
-    update = dot(gated, ow_ref[...])
-    next_pair = pair_ref[...].reshape(T, C).astype(F32) + update
-    us_ref[...] = next_pair.astype(BF16).reshape(2, NB, BR, C)
-    d_gate = dgated_ref[...] * attended * gating * (1.0 - gating)
-    dproj_ref[:, 0:HD] = (dq_ref[...].reshape(T, HD) * scaling).astype(BF16)
-    for r in range(2):
-        rows = slice(r * N, (r + 1) * N)
-        dproj_ref[rows, HD : 2 * HD] = jnp.transpose(dkt_ref[r]).astype(BF16)
-        dproj_ref[rows, 2 * HD : 3 * HD] = jnp.transpose(dvt_ref[r]).astype(BF16)
-    dproj_ref[:, 3 * HD :] = d_gate.astype(BF16)
-    proj_part = dot(normed_ref[...], dproj_ref[...], TN)
-    out_part = dot(gated, cot_ref[...].reshape(T, C), TN)
-    wfull_ref[0] = proj_part[:, 0 : 3 * HD].reshape(16, 8, 3 * HD).astype(BF16)
-    wfull_ref[1, :, :, 0:HD] = proj_part[:, 3 * HD :].reshape(16, 8, HD).astype(BF16)
-    wfull_ref[1, :, :, HD : 2 * HD] = out_part.reshape(16, 8, HD).astype(BF16)
-    wfull_ref[1, :, :, 2 * HD :] = jnp.zeros((16, 8, HD), BF16)
-    wc = copy(wfull_ref.at[1 - c], wrc_ref, wc_s, wc_r, partner)
-    wc.start()
-
-    chain_sums = jnp.zeros((8, C), F32)
-    lane = lax.broadcasted_iota(jnp.int32, (8, C), 1)
-    row = lax.broadcasted_iota(jnp.int32, (8, C), 0)
-    for h in range(H):
-        value = jnp.sum(dbias_ref[h] * same_ref[...], axis=0, keepdims=True)
-        value = jnp.sum(value, axis=1, keepdims=True)
-        chain_sums = jnp.where((row == H) & (lane == h), value, chain_sums)
-
-    wc.wait()
-    own_half = wfull_ref[c].astype(F32) + wrc_ref[...].astype(F32)
-    wsa_ref[...] = own_half.reshape(NB, 128 // NB, 3 * HD).astype(BF16)
+    d_gate = dgated_ref[...].reshape(rows_all, HD) * attended * gating * (1.0 - gating)
+    d_query = dq_ref[...].reshape(rows_all, HD) * scaling
+    mine = lax.broadcasted_iota(jnp.int32, (rows_all, HD), 1) // HW == c
+    both = jnp.where(mine, d_query, pltpu.roll(d_gate, HW, 1))
+    dproj_ref[:, 0:HD] = both.astype(BF16)
+    for core in range(NC):
+        for r in range(2):
+            rows = slice((core * 2 + r) * N, (core * 2 + r + 1) * N)
+            dproj_ref[rows, HD:] = jnp.transpose(dkv_ref[core, r]).astype(BF16)
+    normed_all = rows_ref[z].reshape(rows_all, C)
+    proj_part = dot(normed_all, dproj_ref[...], TN)
+    outp_ref[...] = dot(gated, cot_ref[...].reshape(rows_all, C), TN)
+    out_part = outp_ref[pl.ds(pl.multiple_of(c * HW, HW), HW), :]
+    out_part = jnp.concatenate([out_part, jnp.zeros((C - HW, C), F32)], axis=0)
+    wsa = jnp.concatenate([proj_part, out_part], axis=1)
+    wsa_ref[...] = wsa.reshape(NB, C // NB, 3 * HD).astype(BF16)
     for b in plane:
         send(wsa_ref.at[b], wra_ref.at[yx], wa_s, wa_r, yx_peer(b))
     later(wra_ref.at[pl.ds(0, NB - 1)], wa_s)
     wra_ref[yx] = wsa_ref[yx]
 
+    update = dot(gated, ow_ref[...])
+    u32_ref[...] = update.reshape(NC, T, C)
+    u16_ref[...] = u32_ref[1 - c].astype(BF16)
+    send(u16_ref, up_ref, up_s, up_r, partner)
+    later(u16_ref, up_s)
+
+    chain_sums = jnp.zeros((8, C), F32)
+    lane = lax.broadcasted_iota(jnp.int32, (8, C), 1)
+    row = lax.broadcasted_iota(jnp.int32, (8, C), 0)
+    for t in range(HC):
+        value = jnp.sum(dbias_ref[t] * same_ref[...], axis=0, keepdims=True)
+        value = jnp.sum(value, axis=1, keepdims=True)
+        chain_sums = jnp.where((row == H) & (lane == near + t), value, chain_sums)
+
+    arrived(up_ref, up_r)
+    update = u32_ref[c] + up_ref[...].astype(F32)
+    next_pair = pair_ref[...].reshape(T, C).astype(F32) + update
+    us_ref[...] = next_pair.astype(BF16).reshape(2, NB, BR, C)
     for b in plane:
         send(us_ref.at[:, b], ub_ref.at[yx], ua_s, ua_r, yx_peer(b))
     later(ub_ref.at[pl.ds(0, NB - 1)], ua_s)
@@ -399,7 +403,7 @@
         zz = lax.rem(z + d, NZ)
         arrived(rows_ref.at[zz, c], nz_r.at[number])
         row_slot(zz)
-    later(rows_ref.at[:, c], nc_s)
+    later(rows_ref.at[pl.ds(0, NZ - 1), c], nc_s)
 
     total = sa_ref[:, yx].astype(F32)
     arrived(ra_ref.at[pl.ds(0, NB - 1)], rsa_r)
@@ -414,7 +418,7 @@
     parts = jnp.zeros((8, BR * N), F32)
     for t in range(HC):
         parts = jnp.where(row == near + t, wide[t : t + 1], parts)
-    arrived(rows_ref.at[:, 1 - c], nc_r)
+    arrived(rows_ref.at[pl.ds(0, NZ - 1), 1 - c], nc_r)
     small = dot(parts.astype(BF16), rows_ref[...].reshape(BR * N, C))
     t0_ref[zc] = small + chain_sums
     for g in column:
@@ -447,7 +451,18 @@
     later(ur_ref.at[pl.ds(0, G - 1)], uz_s)
     ur_ref[zc] = uz_ref[zc]
 
-    d_normed = dot(dproj_ref[...], w_ref[...], NT)
+    first = lax.broadcasted_iota(jnp.int32, (C, HD), 1) < HW
+    own_lanes = lax.broadcasted_iota(jnp.int32, (C, HD), 1) // HW == c
+    weights = [w_ref[:, i * HD : (i + 1) * HD].astype(F32) for i in range(4)]
+    swapped = [pltpu.roll(v, HW, 1) for v in weights]
+    pick_k = jnp.where(c == 0, weights[1], swapped[1])
+    pick_v = jnp.where(c == 0, swapped[2], weights[2])
+    wc_ref[:, 0:HD] = jnp.where(own_lanes, weights[0], swapped[3]).astype(BF16)
+    wc_ref[:, HD:] = jnp.where(first, pick_k, pick_v).astype(BF16)
+    u32_ref[...] = dot(dproj_ref[...], wc_ref[...], NT).reshape(NC, T, C)
+    d16_ref[...] = u32_ref[1 - c].astype(BF16)
+    send(d16_ref, dn_ref, dn_s, dn_r, partner)
+    later(d16_ref, dn_s)
 
     arrived(t0_ref.at[pl.ds(0, G - 1)], t0_r)
     small = t0_ref[0]
@@ -485,7 +500,8 @@
     d_bias = jnp.concatenate(d_bias, axis=1)
     d_bias = jnp.concatenate([d_bias, jnp.zeros((8 - H, T), F32)], axis=0).astype(BF16)
 
-    d_normed = d_normed + dot(d_bias, bwt, TN)
+    arrived(dn_ref, dn_r)
+    d_normed = u32_ref[c] + dn_ref[...].astype(F32) + dot(d_bias, bwt, TN)
     standard = std_ref[...]
     mean_grad = jnp.mean(d_normed, axis=-1, keepdims=True)
     mean_cross = jnp.mean(d_normed * standard, axis=-1, keepdims=True)
@@ -515,9 +531,6 @@
     wgc.wait_send()
     for d in drains:
         d.wait_send()
-    for t in range(HC):
-        rsc(t).wait_send()
-        handed(far, t).wait_send()
 
 
 def scratch(grid, N):
@@ -533,37 +546,31 @@
         V((C, 4 * HD), BF16),
         V((H, C), BF16),
         V((HD, C), BF16),
-        V((2, N, C), BF16),
+        V((NC, 2, N, C), BF16),
         V((T, C), F32),
         V((T, C), F32),
-        V((T, C), BF16),
-        V((T, HD), BF16),
-        V((T, HD), BF16),
-        V((T, HD), BF16),
-        V((T, HD), BF16),
-        V((2, HD, N), BF16),
-        V((2, HD, N), BF16),
-        V((T, HD), F32),
-        V((T, HD), F32),
-        V((2, N, HD), F32),
-        V((2, N, HD), F32),
-        V((2, HD, N), F32),
-        V((2, HD, N), F32),
+        V((NC, T, HD), BF16),
+        V((NC, T, HD), BF16),
+        V((NC, T, HD), BF16),
+        V((NC, T, HD), BF16),
+        V((NC, 2, HD, N), BF16),
+        V((NC, 2, HD, N), BF16),
+        V((NC, T, HD), F32),
+        V((NC, T, HD), F32),
+        V((NC, 2, N, HD), F32),
+        V((NC, 2, N, HD), F32),
+        V((NC, 2, HD, N), F32),
         V((N, N), F32),
-        V((H, N, N), F32),
-        V((T, 4 * HD), BF16),
-        V((2, H, N, N), F32),
-        V((2, H, N, N), F32),
+        V((HC, N, N), F32),
+        V((NC * T, 2 * HD), BF16),
+        V((HC, NC, 2, N, N), F32),
+        V((HC, NC, 2, N, N), F32),
         V((G, 2 * H, N), BF16),
-        V((H, NB, BR, N), BF16),
-        V((HC, NB, BR, N), BF16),
         V((HC, NB, BR, N), BF16),
         V((HC, NB, BR, N), BF16),
         V((NB, HC, BR, N), BF16),
         V((G, 2 * HC, N), F32),
         V((G, 2 * HC, N), F32),
-        V((NC, 16, 8, 3 * HD), BF16),
-        V((16, 8, 3 * HD), BF16),
         V((NB, WR, 3 * HD), BF16),
         V((NB, WR, 3 * HD), BF16),
         V((NZ, WR, 3 * HD), BF16),
@@ -576,13 +583,17 @@
         V((G, 8, C), F32),
         V((NB, 8, C), F32),
         V((NZ, NC, T, C), BF16),
+        V((NC, T, C), F32),
+        V((T, C), BF16),
+        V((T, C), BF16),
+        V((T, C), BF16),
+        V((T, C), BF16),
+        V((C, 2 * HD), BF16),
+        V((HD, C), F32),
     ]
     dma = pltpu.SemaphoreType.DMA
-    pairs = [None] * 16
-    pairs[3] = pairs[4] = (HC,)
     buffers.append(dma((8,)))
-    for shape in pairs[1:16]:
-        buffers += [dma if shape is None else dma(shape)] * 2
+    buffers += [dma] * (2 * 16)
     buffers += [dma, dma((NZ,)), dma, dma]
     return buffers
 
@@ -592,11 +603,16 @@
     npt_o[...] = npt_ref[...].reshape(2, N, C)
     pg_o[...] = pg_ref[...].reshape(2, N, C)
     scale = 1.0 / N
-    first = wag_ref[0].astype(F32).reshape(C, 3 * HD) * scale
-    second = wag_ref[1].astype(F32).reshape(C, 3 * HD) * scale
-    wg_o[:, 0 : 3 * HD] = first
-    wg_o[:, 3 * HD :] = second[:, 0:HD]
-    og_o[...] = second[:, HD : 2 * HD]
+    width = HD // wag_ref.shape[0]
+    cores = [wag_ref[i].astype(F32).reshape(C, 3 * HD) * scale for i in range(2)]
+    pairs = [[v[:, i * HD : (i + 1) * HD] for v in cores] for i in range(2)]
+    swapped = [[pltpu.roll(v, width, 1) for v in pair] for pair in pairs]
+    first = lax.broadcasted_iota(jnp.int32, (C, HD), 1) < width
+    wg_o[:, 0:HD] = jnp.where(first, pairs[0][0], pairs[0][1])
+    wg_o[:, HD : 2 * HD] = jnp.where(first, pairs[1][0], swapped[1][1])
+    wg_o[:, 2 * HD : 3 * HD] = jnp.where(first, swapped[1][0], pairs[1][1])
+    wg_o[:, 3 * HD :] = jnp.where(first, swapped[0][0], swapped[0][1])
+    og_o[...] = jnp.concatenate([v[0:width, 2 * HD :] for v in cores], axis=0)
     bg_o[...] = small_ref[0:H, :]
     cg_o[...] = small_ref[H : H + 1, 0:H]
 

time: 44.2 us -> 42.2 us (0.955)
  Pallas kernels: 43.5 us -> 41.5 us
    pallas_call x1, Pallas kernels: 42.6 us -> 40.6 us  [body(): pl.pallas_call(functools.partial(kernel, grid, N), out_shape=(pltpu.VMEM(...]
where the time goes in v5:
time: 42.2 us; the launch traced here: 42.1 us
  Pallas kernels  41.5 us (98%)
  between operations  0.64 us (2%)
    pallas_call x1, Pallas kernels, body(): pl.pallas_call(functools.partial(kernel, grid, N), out_shape=(pltpu.VMEM(...  40.6 us
    pallas_call x1, Pallas kernels, body(): pl.pallas_call(finish, out_shape=(jax.ShapeDtypeStruct((2, N, C), F32), j...  0.91 us

profile of v5, /device:TPU:1, one launch (start us, length us, event | category | flops | bytes accessed | tf_op | source)
XLA Modules:
  0.0 42.1 jit_solution(12152473906913167385)
XLA Ops:
  0.6 40.6 %shard_map.127 = (f32[512,128]{1,0:T(8,128)S(1)}, bf16[512,128]{1,0:T(8,128)(2,1)S(1)}, bf16[2,16,8,384]{3,2,1,0:T(8,128)(2,1)S(1)}, f32[8,128]{1,0:T(8,128)S(1)}) custom-call(f32[1,4]{1,0:T(1,128)} %bitcast.9, bf16[2,256,128]{2,1,0:T(8,128)(2,1)} %pair_hbm.1, s32[1,256]{1,0:T(1,128)} %bitcast.6, s32[1,256]{1,0:T(1,128)} %bitcast.7, bf16[128,512]{1,0:T(8,128)(2,1)} %w_hbm.1, ...), custom_call_target="tpu_custom_call" | custom-call | tf_op jit(solution)/shard_map/pallas_call | solution.py:627
  41.2 0.9 %shard_map.128 = (f32[2,256,128]{2,1,0:T(8,128)}, bf16[2,256,128]{2,1,0:T(8,128)(2,1)}, f32[128,512]{1,0:T(8,128)}, f32[4,128]{1,0:T(4,128)}, f32[1,4]{1,0:T(1,128)}, /*index=5*/f32[128,128]{1,0:T(8,128)}) custom-call(f32[512,128]{1,0:T(8,128)S(1)} %get-tuple-element.16.npt_ref, bf16[512,128]{1,0:T(8,128)(2,1)S(1)} %get-tuple-element.17.pg_ref, ...), custom_call_target="tpu_custom_call" | custom-call | tf_op jit(solution)/shard_map/pallas_call | solution.py:649

commit v6 on v5

--- a/solution.py
+++ b/solution.py
@@ -57,7 +57,7 @@
     qt_ref,
     dat_ref,
     gate_ref,
-    dgated_ref,
+    dgate_ref,
     att_ref,
     dq_ref,
     dkv_ref,
@@ -90,7 +90,8 @@
     d16_ref,
     dn_ref,
     wc_ref,
-    outp_ref,
+    nt_ref,
+    ct_ref,
     in_s,
     slot_s,
     slot_r,
@@ -252,8 +253,8 @@
         gating = jax.nn.sigmoid(projected[:, 3 * HD :])
         gate_ref[core] = gating
         d_gated = dot(cot_ref[core].reshape(T, C), ow_ref[...], NT)
-        dgated_ref[core] = d_gated
         da32 = d_gated * gating
+        dgate_ref[core] = da32 * (1.0 - gating)
         da_ref[core] = da32.astype(BF16)
         for r in range(2):
             rows = slice(r * N, (r + 1) * N)
@@ -264,6 +265,11 @@
     arrived(rows_ref.at[z, 1 - c], pn_r)
     arrived(cot_ref.at[1 - c], pc_r)
     project(1 - c)
+    for core in range(NC):
+        rows = slice(core * T, (core + 1) * T)
+        nt_ref[:, rows] = jnp.transpose(rows_ref[z, core].astype(F32)).astype(BF16)
+        grads = cot_ref[core].reshape(T, C).astype(F32)
+        ct_ref[:, rows] = jnp.transpose(grads).astype(BF16)
 
     part = rows_ref.at[z, c]
     round_z = [lax.rem(z + d, NZ) for d in ((2, 1, 3) if NZ == 4 else range(1, NZ))]
@@ -305,18 +311,18 @@
         pick = (at == lax.broadcasted_iota(jnp.int32, (BR, G * 2 * H), 1)).astype(BF16)
         bias_ref[t, yx] = dot(pick, gathered).astype(BF16)
 
-    for b in plane:
-        send(bias_ref.at[:, yx], bias_ref.at[:, yx], ag_s, ag_r, yx_peer(b))
-    most = bias_ref.at[:, pl.ds(0, NB - 1)]
-    later(most, ag_s)
-
-    arrived(most, ag_r)
+    for t in range(HC):
+        part = bias_ref.at[t, yx]
+        for b in plane:
+            send(part, part, ag_s, ag_r.at[t], yx_peer(b))
+    later(bias_ref.at[:, pl.ds(0, NB - 1)], ag_s)
 
     att_ref[...] = jnp.zeros((NC, 2, N, HD), F32)
     dq_ref[...] = jnp.zeros((NC, 2, N, HD), F32)
 
     @pl.loop(0, HC)
     def _(t):
+        arrived(bias_ref.at[t, pl.ds(0, NB - 1)], ag_r.at[t])
         h = near + t
         own = head_of == h
         bias = bias_ref[t].reshape(N, N).astype(F32)
@@ -355,7 +361,7 @@
     attended = att_ref[...].reshape(rows_all, HD)
     gating = gate_ref[...].reshape(rows_all, HD)
     gated = (gating * attended).astype(BF16)
-    d_gate = dgated_ref[...].reshape(rows_all, HD) * attended * gating * (1.0 - gating)
+    d_gate = dgate_ref[...].reshape(rows_all, HD) * attended
     d_query = dq_ref[...].reshape(rows_all, HD) * scaling
     mine = lax.broadcasted_iota(jnp.int32, (rows_all, HD), 1) // HW == c
     both = jnp.where(mine, d_query, pltpu.roll(d_gate, HW, 1))
@@ -364,13 +370,10 @@
         for r in range(2):
             rows = slice((core * 2 + r) * N, (core * 2 + r + 1) * N)
             dproj_ref[rows, HD:] = jnp.transpose(dkv_ref[core, r]).astype(BF16)
-    normed_all = rows_ref[z].reshape(rows_all, C)
-    proj_part = dot(normed_all, dproj_ref[...], TN)
-    outp_ref[...] = dot(gated, cot_ref[...].reshape(rows_all, C), TN)
-    out_part = outp_ref[pl.ds(pl.multiple_of(c * HW, HW), HW), :]
-    out_part = jnp.concatenate([out_part, jnp.zeros((C - HW, C), F32)], axis=0)
-    wsa = jnp.concatenate([proj_part, out_part], axis=1)
-    wsa_ref[...] = wsa.reshape(NB, C // NB, 3 * HD).astype(BF16)
+    proj_part = dot(nt_ref[...], dproj_ref[...])
+    out_part = dot(ct_ref[...], gated)
+    wsa_ref[:, :, 0 : 2 * HD] = proj_part.reshape(NB, C // NB, 2 * HD).astype(BF16)
+    wsa_ref[:, :, 2 * HD :] = out_part.reshape(NB, C // NB, HD).astype(BF16)
     for b in plane:
         send(wsa_ref.at[b], wra_ref.at[yx], wa_s, wa_r, yx_peer(b))
     later(wra_ref.at[pl.ds(0, NB - 1)], wa_s)
@@ -412,6 +415,15 @@
     for g in range(G):
         for jl in range(2):
             sz_ref[g, jl * HC : (jl + 1) * HC, :] = total[:, 2 * g + jl, :]
+
+    arrived(wra_ref.at[pl.ds(0, NB - 1)], wa_r)
+    wsum = wra_ref[0].astype(F32)
+    for b in range(1, NB):
+        wsum = wsum + wra_ref[b].astype(F32)
+    wrz_ref[z] = wsum.astype(BF16)
+    for zz in others(z, NZ):
+        send(wrz_ref.at[z], wrz_ref.at[z], wz_s, wz_r, z_peer(zz))
+    later(wrz_ref.at[pl.ds(0, NZ - 1)], wz_s)
 
     wide = jnp.concatenate([total[:, i, :] for i in range(BR)], axis=1)
     row = lax.broadcasted_iota(jnp.int32, (8, BR * N), 0)
@@ -424,15 +436,6 @@
     for g in column:
         send(t0_ref.at[zc], t0_ref.at[zc], t0_s, t0_r, zc_peer(g))
     later(t0_ref.at[pl.ds(0, G - 1)], t0_s)
-
-    arrived(wra_ref.at[pl.ds(0, NB - 1)], wa_r)
-    wsum = wra_ref[0].astype(F32)
-    for b in range(1, NB):
-        wsum = wsum + wra_ref[b].astype(F32)
-    wrz_ref[z] = wsum.astype(BF16)
-    for zz in others(z, NZ):
-        send(wrz_ref.at[z], wrz_ref.at[z], wz_s, wz_r, z_peer(zz))
-    later(wrz_ref.at[pl.ds(0, NZ - 1)], wz_s)
 
     for g in column:
         send(sz_ref.at[g], rz_ref.at[zc], rsz_s, rsz_r, zc_peer(g))
@@ -464,6 +467,24 @@
     send(d16_ref, dn_ref, dn_s, dn_r, partner)
     later(d16_ref, dn_s)
 
+    arrived(wrz_ref.at[pl.ds(0, NZ - 1)], wz_r)
+    wsum = wrz_ref[0].astype(F32)
+    for zz in range(1, NZ):
+        wsum = wsum + wrz_ref[zz].astype(F32)
+    wag_ref[c, yx] = wsum.astype(BF16)
+
+    part = wag_ref.at[c, yx]
+    half = NB // 2
+    for number, b in enumerate(plane):
+        send(part, part, wga_s, wga_r.at[number // half], yx_peer(b))
+    later(wag_ref.at[c, pl.ds(0, NB - 1)], wga_s)
+
+    def pass_on(b):
+        part = wag_ref.at[c, b]
+        send(part, part, wgc_s, wgc_r, partner)
+
+    pass_on(yx)
+
     arrived(t0_ref.at[pl.ds(0, G - 1)], t0_r)
     small = t0_ref[0]
     for g in range(1, G):
@@ -472,18 +493,6 @@
     for b in plane:
         send(t1_ref.at[yx], t1_ref.at[yx], t1_s, t1_r, yx_peer(b))
     later(t1_ref.at[pl.ds(0, NB - 1)], t1_s)
-
-    arrived(wrz_ref.at[pl.ds(0, NZ - 1)], wz_r)
-    wsum = wrz_ref[0].astype(F32)
-    for zz in range(1, NZ):
-        wsum = wsum + wrz_ref[zz].astype(F32)
-    wag_ref[c, yx] = wsum.astype(BF16)
-
-    part = wag_ref.at[c, yx]
-    for b in plane:
-        send(part, part, wga_s, wga_r, yx_peer(b))
-    most = wag_ref.at[c, pl.ds(0, NB - 1)]
-    later(most, wga_s)
 
     arrived(rz_ref.at[pl.ds(0, G - 1)], rsz_r)
     sums = []
@@ -506,29 +515,31 @@
     mean_grad = jnp.mean(d_normed, axis=-1, keepdims=True)
     mean_cross = jnp.mean(d_normed * standard, axis=-1, keepdims=True)
     pair_grad = (d_normed - mean_grad - standard * mean_cross) * inv_ref[...]
-    pg_o[...] = pair_grad.astype(BF16)
-
-    arrived(most, wga_r)
-    part = wag_ref.at[c]
-    wgc = copy(part, part, wgc_s, wgc_r, partner)
-    wgc.start()
+    pg_o[...] = pair_grad.astype(BF16).reshape(2, N, C)
+
+    back = [lax.rem(y - i + NY, NY) * NX + lax.rem(x - j + NX, NX) for i, j in steps]
+    for group in (1, 0):
+        blocks = back[group * half : (group + 1) * half]
+        arrived(wag_ref.at[c, pl.ds(0, len(blocks))], wga_r.at[group])
+        for b in blocks:
+            pass_on(b)
+    later(wag_ref.at[c], wgc_s)
 
     arrived(ur_ref.at[pl.ds(0, G - 1)], uz_r)
     for g in range(G):
         for jl in range(2):
             for r in range(2):
-                start = jl * N + 2 * g + r
-                npt_o[pl.ds(start, NB, stride=BR), :] = ur_ref[g, jl, r].astype(F32)
+                start = 2 * g + r
+                npt_o[jl, pl.ds(start, NB, stride=BR), :] = ur_ref[g, jl, r].astype(F32)
 
     arrived(t1_ref.at[pl.ds(0, NB - 1)], t1_r)
     small = t1_ref[0]
     for b in range(1, NB):
         small = small + t1_ref[b]
     small_o[...] = small * (1.0 / N)
-    wgc.wait_recv()
+    arrived(wag_ref.at[1 - c], wgc_r)
     wag_o[...] = wag_ref[...]
 
-    wgc.wait_send()
     for d in drains:
         d.wait_send()
 
@@ -589,19 +600,23 @@
         V((T, C), BF16),
         V((T, C), BF16),
         V((C, 2 * HD), BF16),
-        V((HD, C), F32),
+        V((C, NC * T), BF16),
+        V((C, NC * T), BF16),
     ]
     dma = pltpu.SemaphoreType.DMA
     buffers.append(dma((8,)))
-    buffers += [dma] * (2 * 16)
+    singles = [dma] * (2 * 16)
+    singles[3] = dma((HC,))
+    singles[13] = dma((2,))
+    buffers += singles
     buffers += [dma, dma((NZ,)), dma, dma]
     return buffers
 
 
 def finish(npt_ref, pg_ref, wag_ref, small_ref, npt_o, pg_o, wg_o, bg_o, cg_o, og_o):
     N = npt_o.shape[1]
-    npt_o[...] = npt_ref[...].reshape(2, N, C)
-    pg_o[...] = pg_ref[...].reshape(2, N, C)
+    npt_o[...] = npt_ref[...]
+    pg_o[...] = pg_ref[...]
     scale = 1.0 / N
     width = HD // wag_ref.shape[0]
     cores = [wag_ref[i].astype(F32).reshape(C, 3 * HD) * scale for i in range(2)]
@@ -612,7 +627,8 @@
     wg_o[:, HD : 2 * HD] = jnp.where(first, pairs[1][0], swapped[1][1])
     wg_o[:, 2 * HD : 3 * HD] = jnp.where(first, swapped[1][0], pairs[1][1])
     wg_o[:, 3 * HD :] = jnp.where(first, swapped[0][0], swapped[0][1])
-    og_o[...] = jnp.concatenate([v[0:width, 2 * HD :] for v in cores], axis=0)
+    out_t = jnp.where(first, cores[0][:, 2 * HD :], cores[1][:, 2 * HD :])
+    og_o[...] = jnp.transpose(out_t)
     bg_o[...] = small_ref[0:H, :]
     cg_o[...] = small_ref[H : H + 1, 0:H]
 
@@ -627,8 +643,8 @@
     results = pl.pallas_call(
         functools.partial(kernel, grid, N),
         out_shape=(
-            pltpu.VMEM((2 * N, C), F32),
-            pltpu.VMEM((2 * N, C), BF16),
+            pltpu.VMEM((2, N, C), F32),
+            pltpu.VMEM((2, N, C), BF16),
             pltpu.VMEM((NC, NX * NY, 128 // (NX * NY), 3 * HD), BF16),
             pltpu.VMEM((8, C), F32),
         ),

time: 42.2 us -> 41.4 us (0.981)
  Pallas kernels: 41.5 us -> 40.7 us
    pallas_call x1, Pallas kernels: 40.6 us -> 39.7 us  [body(): pl.pallas_call(functools.partial(kernel, grid, N), out_shape=(pltpu.VMEM(...]
where the time goes in v6:
time: 41.4 us; the launch traced here: 41.3 us
  Pallas kernels  40.7 us (98%)
  between operations  0.64 us (2%)
    pallas_call x1, Pallas kernels, body(): pl.pallas_call(functools.partial(kernel, grid, N), out_shape=(pltpu.VMEM(...  39.7 us
    pallas_call x1, Pallas kernels, body(): pl.pallas_call(finish, out_shape=(jax.ShapeDtypeStruct((2, N, C), F32), j...  0.98 us

profile of v6, /device:TPU:1, one launch (start us, length us, event | category | flops | bytes accessed | tf_op | source)
XLA Modules:
  0.0 41.3 jit_solution(4703817433744014137)
XLA Ops:
  0.6 39.7 %shard_map.127 = (f32[2,256,128]{2,1,0:T(8,128)S(1)}, bf16[2,256,128]{2,1,0:T(8,128)(2,1)S(1)}, bf16[2,16,8,384]{3,2,1,0:T(8,128)(2,1)S(1)}, f32[8,128]{1,0:T(8,128)S(1)}) custom-call(f32[1,4]{1,0:T(1,128)} %bitcast.9, bf16[2,256,128]{2,1,0:T(8,128)(2,1)} %pair_hbm.1, s32[1,256]{1,0:T(1,128)} %bitcast.6, s32[1,256]{1,0:T(1,128)} %bitcast.7, ...), custom_call_target="tpu_custom_call" | custom-call | tf_op jit(solution)/shard_map/pallas_call | solution.py:643
  40.4 1.0 %shard_map.128 = (f32[2,256,128]{2,1,0:T(8,128)}, bf16[2,256,128]{2,1,0:T(8,128)(2,1)}, f32[128,512]{1,0:T(8,128)}, f32[4,128]{1,0:T(4,128)}, f32[1,4]{1,0:T(1,128)}, /*index=5*/f32[128,128]{1,0:T(8,128)}) custom-call(f32[2,256,128]{2,1,0:T(8,128)S(1)} %get-tuple-element.16.npt_ref, bf16[2,256,128]{2,1,0:T(8,128)(2,1)S(1)} %get-tuple-element.17.pg_ref, ...), custom_call_target="tpu_custom_call" | custom-call | tf_op jit(solution)/shard_map/pallas_call | solution.py:665
